TPU v7x, 32 devices: a whole 2x2x4 slice. The times are simulated.
32 devices in a mesh: wave: 8 (over y, x, core), lev: 4 (over z).
Axes of the slice: x: 2, y: 2, z: 4, core: 2. Of those that a mesh axis runs over, the one named last changes fastest.
Arguments:
- spectra: bfloat16 [2, 128, 1280, 1280], P(None, 'lev', 'wave'), may hold values from -6 to 6
- polynomials: bfloat16 [1280, 1280, 32], P('wave'), may hold values from -0.0048828125 to 0.0048828125
- wave_order: int32 [1280], replicated, may hold values from 0 to 1279, as said below
- row_cutoff: int32 [64], replicated, may hold values from 320 to 1280
Outputs:
- grid: bfloat16 [64, 128, 5120], P(('wave', 'lev'))
Inputs may be any that keep to these rules, and one draw needn't show every extreme that they name: `wave_order`: a permutation of the wavenumbers 0 to 1279; slots 2 s and 2 s + 1 hold wavenumbers that add up to 1279.
All inputs are finite; a program needn't handle non-finite values.
Results may differ from a plain program's by a relative error of at most 0.0055.
Values may be sent and summed in bfloat16 or wider, within the bound.
No kernel may reach another device: no remote copies, remote signals or barrier semaphores. Data moves between devices by JAX's collectives and lax.ppermute only.
A program may use at most 448 MiB of HBM per device.

v0:
```python
import math

import jax
import jax.numpy as jnp
from jax import lax
from jax.sharding import PartitionSpec as P

NLON = 5120


def make_phases(wave_order):
    inner_count = 128
    outer_count = NLON // inner_count
    scale = 2.0 * math.pi / NLON
    inner = jnp.arange(inner_count, dtype=jnp.int32)
    outer = jnp.arange(outer_count, dtype=jnp.int32)
    first = (wave_order[:, None] * inner[None, :] % NLON).astype(jnp.float32) * scale
    second = (wave_order[:, None] * (outer[None, :] * inner_count) % NLON).astype(
        jnp.float32
    ) * scale
    cos_first = jnp.cos(first)[None, :, None, :]
    sin_first = jnp.sin(first)[None, :, None, :]
    cos_second = jnp.cos(second)
    sin_second = jnp.sin(second)
    weights = jnp.where(wave_order == 0, 1.0, 2.0).astype(jnp.float32)[None, :, None, None]
    with_cos = jnp.stack([cos_second, -sin_second])[..., None]
    with_sin = jnp.stack([-sin_second, -cos_second])[..., None]
    table = weights * (with_cos * cos_first + with_sin * sin_first)
    return table.astype(jnp.bfloat16).reshape(2, wave_order.shape[0], NLON)


def local(spectra, polynomials, wave_order, row_cutoff):
    slot_count = polynomials.shape[0]
    waves = polynomials.shape[1]
    first_slot = lax.axis_index("wave") * slot_count
    local_waves = lax.dynamic_slice_in_dim(wave_order, first_slot, slot_count, 0)
    degrees = jnp.arange(waves, dtype=jnp.int32)
    usable = degrees[None, :] <= (waves - 1 - local_waves)[:, None]
    coeffs = jnp.where(usable[None, None], spectra, jnp.zeros((), jnp.bfloat16))
    parity_sign = jnp.where(degrees % 2 == 0, 1.0, -1.0).astype(jnp.bfloat16)
    flipped = coeffs * parity_sign
    northern = jnp.einsum("rvkj,kji->krvi", coeffs, polynomials, preferred_element_type=jnp.float32)
    southern = jnp.einsum(
        "rvkj,kji->krvi", flipped, polynomials, preferred_element_type=jnp.float32
    )
    fourier = jnp.concatenate([northern, southern], axis=3).astype(jnp.bfloat16)
    phases = make_phases(wave_order)
    rows_per_wave = fourier.shape[3] // lax.axis_size("wave")
    level_count = lax.axis_size("lev")
    rows_here = rows_per_wave // level_count
    cutoffs = lax.dynamic_slice_in_dim(
        row_cutoff, lax.axis_index("wave") * rows_per_wave, rows_per_wave, 0
    )
    retained = wave_order[:, None] < cutoffs[None, :]
    kept = jnp.where(
        retained[:, None, None, :],
        lax.all_to_all(fourier, "wave", split_axis=3, concat_axis=0, tiled=True),
        jnp.zeros((), jnp.bfloat16),
    )
    shaped = kept.reshape(kept.shape[0], kept.shape[1], kept.shape[2], level_count, rows_here)
    longitudes = jnp.einsum(
        "ksvgq,skx->gqvx", shaped, phases, preferred_element_type=jnp.float32
    ).astype(jnp.bfloat16)
    arrived = lax.all_to_all(longitudes, "lev", split_axis=0, concat_axis=2, tiled=True)
    return arrived.reshape(rows_here, arrived.shape[2], arrived.shape[3])


def solution(mesh):
    in_specs = (P(None, "lev", "wave", None), P("wave", None, None), P(), P())
    out_specs = P(("wave", "lev"), None, None)
    return jax.shard_map(local, mesh=mesh, in_specs=in_specs, out_specs=out_specs, check_vma=False)
```

profile of v0, /device:TPU:1, one launch (start us, length us, event | category | flops | bytes accessed | tf_op | source)
XLA Modules:
  0.0 415.5 jit_solution(4887767515928801274)
XLA Ops:
  0.0 0.8 dynamic-slice_subtract_fusion
  0.8 0.2 iota_compare_fusion
  1.0 25.0 %broadcast_multiply_fusion = (bf16[2,32,160,1280]{3,2,1,0:T(8,128)(2,1)}, bf16[2,32,160,1280]{3,2,1,0:T(8,128)(2,1)}) fusion(bf16[1280]{0:T(1024)(128)(2,1)S(1)} %select_convert_fusion, bf16[2,32,160,1280]{3,2,1,0:T(8,128)(2,1)} %param.4, pred[160,1280]{1,0:T(8,128)(4,1)S(1)} %iota_compare_fusion), kind=kLoop, calls=%fused_computation.12 | loop fusion | flops 26214400 | bytes 78850560 | tf_op jit(solution)/shard_map/mul | solution.py:41
  25.9 33.0 %fusion.18 = bf16[160,2,32,32]{3,2,1,0:T(8,128)(2,1)S(1)} fusion(bf16[160,1280,32]{1,2,0:T(8,128)(2,1)} %param.5, bf16[2,32,160,1280]{3,2,1,0:T(8,128)(2,1)} %get-tuple-element.6), kind=kOutput, calls=%fused_computation.17 | convolution fusion | flops 839188480 | bytes 39976960 | tf_op jit(solution)/shard_map/rvkj,kji->krvi/dot_general | solution.py:42
  59.0 0.0 copy-start
  59.0 34.0 %fusion.23 = bf16[160,2,32,32]{3,2,1,0:T(8,128)(2,1)} fusion(bf16[160,1280,32]{1,2,0:T(8,128)(2,1)} %param.5, bf16[2,32,160,1280]{3,2,1,0:T(8,128)(2,1)} %get-tuple-element.5), kind=kOutput, calls=%fused_computation.18 | convolution fusion | flops 839188480 | bytes 39976960 | tf_op jit(solution)/shard_map/rvkj,kji->krvi/dot_general | solution.py:43
  92.9 3.2 pad_maximum_fusion
  96.2 5.3 %copy.22 = bf16[160,2,32,64]{0,2,1,3:T(8,128)(2,1)} copy(bf16[160,2,32,64]{3,2,1,0:T(8,128)(2,1)S(1)} %pad_maximum_fusion) | data formatting | bytes 2621440 | tf_op jit(solution)/shard_map/concatenate | solution.py:46
  101.5 5.2 %all-to-all-start = ((bf16[160,2,32,64]{0,2,1,3:T(8,128)(2,1)}), bf16[160,2,32,64]{0,2,1,3:T(8,128)(2,1)}, u32[]{:S(2)}, u32[]{:S(2)}) async-start(bf16[160,2,32,64]{0,2,1,3:T(8,128)(2,1)} %copy.22), calls=%async_computation | async-start | bytes 4194304 | tf_op jit(solution)/shard_map/all_to_all | solution.py:57
  106.7 0.0 copy-done
  106.7 2.7 fusion.36
  109.4 2.8 mul.171
  112.2 9.1 %mul.177 = f32[1280,40,128]{2,1,0:T(8,128)} broadcast(f32[1280,128]{1,0:T(8,128)S(1)} %get-tuple-element.13), dimensions={0,2} | broadcast | bytes 26869760 | tf_op jit(solution)/shard_map/mul | solution.py:28
  121.4 0.0 copy-start.1
  121.4 28.4 %copy_bitcast_fusion = (f32[1280,5120]{1,0:T(8,128)}, f32[1280,5120]{1,0:T(8,128)}) fusion(f32[160,8,40,128]{3,2,1,0:T(8,128)} %bitcast.64, f32[160,8,40,128]{3,2,1,0:T(8,128)S(1)} %bitcast.63), kind=kLoop, calls=%fused_computation.2 | loop fusion | bytes 104857600 | tf_op jit(solution)/shard_map/mul | solution.py:28
  149.8 0.9 fusion.42
  150.7 0.0 copy-done.1
  150.7 0.1 dynamic_slice.6
  150.8 0.1 lt.47
  150.9 0.1 pad_maximum_fusion.1
  151.0 0.4 copy.18
  151.4 17.2 %mul.164 = f32[2,1280,40,128]{3,2,1,0:T(8,128)} broadcast(f32[2,1280,40]{2,1,0:T(8,128)S(1)} %copy.18), dimensions={0,1,2} | broadcast | bytes 52838400 | tf_op jit(solution)/shard_map/mul | solution.py:28
  168.6 53.7 %mul.165 = f32[2,1280,5120]{2,1,0:T(8,128)} reshape(f32[2,1280,40,128]{3,2,1,0:T(8,128)} %mul.164) | data formatting | bytes 104857600 | tf_op jit(solution)/shard_map/mul | solution.py:28
  222.3 0.4 copy.19
  222.7 17.2 %mul.175 = f32[2,1280,40,128]{3,2,1,0:T(8,128)} broadcast(f32[2,1280,40]{2,1,0:T(8,128)S(1)} %copy.19), dimensions={0,1,2} | broadcast | bytes 52838400 | tf_op jit(solution)/shard_map/mul | solution.py:28
  239.9 53.7 %mul.176 = f32[2,1280,5120]{2,1,0:T(8,128)} reshape(f32[2,1280,40,128]{3,2,1,0:T(8,128)} %mul.175) | data formatting | bytes 104857600 | tf_op jit(solution)/shard_map/mul | solution.py:28
  293.6 0.1 broadcast_compare_fusion
  293.7 0.0 all-to-all-done
  293.7 3.0 copy.24
  296.7 2.4 all_to_all.27
  299.1 50.6 %fusion.15 = bf16[4,2,32,5120]{3,2,1,0:T(8,128)(2,1)} fusion(f32[2,1280,5120]{2,1,0:T(8,128)} %mul.176, f32[2,1280,5120]{2,1,0:T(8,128)} %mul.165, f32[1280,5120]{1,0:T(8,128)} %get-tuple-element.14, f32[1280,5120]{1,0:T(8,128)} %get-tuple-element.15, f32[1280]{0:T(1024)S(1)} %compare_select_fusion, bf16[1280,2,32,4,2]{0,2,4,3,1:T(8,128)(2,1)S(1)} %all_to_all.27, ...), kind=kOutput, calls=%fused_computation.15 | convolution fusion | flops 6778388480 | bytes 161233920 | tf_op jit(solution)/shard_map/ksvgq,skx->gqvx/dot_general | solution.py:61
  349.7 64.1 %all_to_all.33 = bf16[4,2,32,5120]{3,2,1,0:T(8,128)(2,1)S(1)} all-to-all(bf16[4,2,32,5120]{3,2,1,0:T(8,128)(2,1)} %fusion.15), channel_id=1, replica_groups=mesh['wave'=8,'lev'=4] {'lev'}, dimensions={0} | all-to-all | bytes 5242880 | tf_op jit(solution)/shard_map/all_to_all | solution.py:64
  413.8 1.7 copy.26
  (3 shorter events, 0.0 us)
Async XLA Ops:
  59.0 47.7 %copy-start = (s32[1280]{0:T(1024)S(1)}, s32[1280]{0:T(1024)}, u32[]{:S(2)}) copy-start(s32[1280]{0:T(1024)} %param.6) | copy-start | bytes 15364
  101.5 192.2 %all-to-all-start = ((bf16[160,2,32,64]{0,2,1,3:T(8,128)(2,1)}), bf16[160,2,32,64]{0,2,1,3:T(8,128)(2,1)}, u32[]{:S(2)}, u32[]{:S(2)}) async-start(bf16[160,2,32,64]{0,2,1,3:T(8,128)(2,1)} %copy.22), calls=%async_computation | async-start | bytes 4194304 | tf_op jit(solution)/shard_map/all_to_all | solution.py:57
  121.4 29.3 %copy-start.1 = (s32[64]{0:T(128)S(1)}, s32[64]{0:T(128)}, u32[]{:S(2)}) copy-start(s32[64]{0:T(128)} %param.7) | copy-start | bytes 772
where the time goes:
time: 420 us; the launch traced here: 416 us
  local copies, waits for them, and re-layouts  196 us (47%)
  matrix products  118 us (28%)
  blocking collectives  64.1 us (15%)
  other arithmetic  32.9 us (8%)
  starting transfers between devices  5.22 us (1%)
    mul x7, local copies, waits for them, and re-layouts, make_phases(): table = weights * (with_cos * cos_first + with_sin * sin_first)  182 us
    all_to_all x1, blocking collectives, local(): lax.all_to_all(longitudes, 'lev', split_axis=0, concat_axis=2, tiled=True)  64.1 us
    dot_general x1, matrix products, local(): jnp.einsum('ksvgq,skx->gqvx', shaped, phases, preferred_element_type=jnp....  50.6 us
    dot_general x1, matrix products, local(): jnp.einsum('rvkj,kji->krvi', flipped, polynomials, preferred_element_type...  34 us
    dot_general x1, matrix products, local(): jnp.einsum('rvkj,kji->krvi', coeffs, polynomials, preferred_element_type=...  33 us
    mul x1, other arithmetic, local(): flipped = coeffs * parity_sign  25 us
  transfers between devices with their start and end apart: 1, of which 0 were waited for; matrix products, arithmetic and copies ran while one was open for 45% of the time, Pallas kernels for 0%

commit v1 on v0

v1 whole, which is shorter than its diff:
```python
import functools
import math

import jax
import jax.numpy as jnp
from jax import lax
from jax.experimental import pallas as pl
from jax.experimental.pallas import tpu as pltpu
from jax.sharding import PartitionSpec as P

NLON = 5120
FOLD = NLON // 2
LANES = 128
GROUP = 8
MIB = 1024 * 1024


def nt_dot(left, right):
    return lax.dot_general(
        left, right, (((1,), (1,)), ((), ())), preferred_element_type=jnp.float32
    )


def legendre_kernel(
    first_slot, wave_ref, cut_ref, coeff_ref, basis_ref, out_ref, lhs, pick, rows
):
    parts, levels, _, degrees = coeff_ref.shape
    half = basis_ref.shape[1]
    series = parts * levels
    step = pl.program_id(0)
    slot = lax.axis_index("wave") * first_slot[0] + first_slot[1] + step * GROUP

    @pl.when(step == 0)
    def _():
        source = lax.broadcasted_iota(jnp.int32, pick.shape, 0) // GROUP
        target = lax.broadcasted_iota(jnp.int32, pick.shape, 1) % series
        pick[...] = (source == target).astype(jnp.bfloat16)

    degree = lax.broadcasted_iota(jnp.int32, (1, degrees), 1)
    sign = (1 - 2 * (degree & 1)).astype(jnp.float32)
    waves = [wave_ref[slot + g] for g in range(GROUP)]
    for g in range(GROUP):
        usable = (degree <= degrees - 1 - waves[g]).astype(jnp.float32)
        basis = basis_ref[g]
        lhs[pl.ds(g * half, half), :] = basis * usable.astype(jnp.bfloat16)
        lhs[pl.ds((GROUP + g) * half, half), :] = basis * (usable * sign).astype(jnp.bfloat16)
    coeffs = coeff_ref[...].reshape(series * GROUP, degrees)
    product = nt_dot(lhs[...], coeffs)
    column_slot = lax.broadcasted_iota(jnp.int32, (1, series * GROUP), 1) % GROUP
    for part in range(2):
        for g in range(GROUP):
            block = product[(part * GROUP + g) * half : (part * GROUP + g + 1) * half, :]
            own = jnp.where(column_slot == g, block, 0.0).astype(jnp.bfloat16)
            rows[pl.ds((part * GROUP + g) * half, half), :] = jnp.dot(
                own, pick[...], preferred_element_type=jnp.float32
            )
    sublane = lax.broadcasted_iota(jnp.int32, (GROUP, LANES), 0)
    lane = lax.broadcasted_iota(jnp.int32, (GROUP, LANES), 1)
    wave_column = jnp.zeros((GROUP, LANES), jnp.int32)
    for g in range(GROUP):
        wave_column = jnp.where(sublane == g, waves[g], wave_column)
    rows_here = LANES // series
    for target in range(out_ref.shape[0]):
        value = jnp.zeros((GROUP, LANES), jnp.float32)
        for r in range(rows_here):
            row = target * rows_here + r
            part, i = divmod(row, half)
            loaded = rows[pl.ds(part * GROUP * half + i, GROUP, stride=half), :]
            keep = (lane // series == r) & (wave_column < cut_ref[row])
            value = jnp.where(keep, loaded, value)
        out_ref[target] = value.astype(jnp.bfloat16)


def legendre(spectra, basis, wave_order, row_cutoff, offset, count, targets):
    parts, levels, slots, degrees = spectra.shape
    half = basis.shape[1]
    series = parts * levels
    first = jnp.array([slots, offset], jnp.int32)
    skip = offset // GROUP
    return pl.pallas_call(
        legendre_kernel,
        out_shape=jax.ShapeDtypeStruct((targets, count, LANES), jnp.bfloat16),
        grid_spec=pltpu.PrefetchScalarGridSpec(
            num_scalar_prefetch=3,
            grid=(count // GROUP,),
            in_specs=[
                pl.BlockSpec((parts, levels, GROUP, degrees), lambda g, *_: (0, 0, g + skip, 0)),
                pl.BlockSpec((GROUP, half, degrees), lambda g, *_: (g + skip, 0, 0)),
            ],
            out_specs=pl.BlockSpec((targets, GROUP, LANES), lambda g, *_: (0, g, 0)),
            scratch_shapes=[
                pltpu.VMEM((2 * GROUP * half, degrees), jnp.bfloat16),
                pltpu.VMEM((series * GROUP, LANES), jnp.bfloat16),
                pltpu.VMEM((2 * GROUP * half, LANES), jnp.float32),
            ],
        ),
        compiler_params=pltpu.CompilerParams(vmem_limit_bytes=32 * MIB),
        cost_estimate=pl.CostEstimate(
            flops=4 * count * half * degrees * series * GROUP,
            bytes_accessed=2 * count * degrees * (series + half),
            transcendentals=0,
        ),
        name="legendre",
    )(first, wave_order, row_cutoff, spectra, basis)


def cos_sin(steps):
    turns = jnp.floor(steps * (1.0 / NLON))
    residue = steps - turns * NLON
    quadrant = jnp.floor(residue * (4.0 / NLON) + 0.5)
    angle = (residue - quadrant * (NLON // 4)) * (2.0 * math.pi / NLON)
    square = angle * angle
    cosine = 1.0 + square * (
        -0.5 + square * (1.0 / 24 + square * (-1.0 / 720 + square * (1.0 / 40320)))
    )
    sine = angle * (
        1.0
        + square * (-1.0 / 6 + square * (1.0 / 120 + square * (-1.0 / 5040 + square / 362880.0)))
    )
    turn = quadrant.astype(jnp.int32)
    odd = (turn & 1) == 1
    flip_cos = ((turn + 1) & 2) == 2
    flip_sin = (turn & 2) == 2
    first = jnp.where(odd, sine, cosine)
    second = jnp.where(odd, cosine, sine)
    return jnp.where(flip_cos, -first, first), jnp.where(flip_sin, -second, second)


def table_kernel(layout, wave_ref, out_ref, *, pairs, slots, offset):
    rows = out_ref.shape[2]
    odd_part = pl.program_id(0)
    top = wave_ref.shape[0] - 1
    sublane = lax.broadcasted_iota(jnp.int32, (GROUP, LANES), 0)
    lane = lax.broadcasted_iota(jnp.int32, (GROUP, LANES), 1).astype(jnp.float32)

    for block in range(rows // GROUP):
        column = jnp.zeros((GROUP, LANES), jnp.int32)
        for g in range(GROUP):
            row = pl.program_id(1) * rows + block * GROUP + g
            group = row // pairs
            wave = wave_ref[group * slots + offset + 2 * (row - group * pairs)]
            wave = jnp.where((wave & 1) == odd_part, wave, top - wave)
            column = jnp.where(sublane == g, wave, column)
        wide = column.astype(jnp.float32)
        weight = jnp.where(column == 0, 1.0, 2.0)
        cos_in, sin_in = cos_sin(wide * lane)
        cos_out, sin_out = cos_sin(wide * (lane * LANES))
        cos_in = cos_in * weight
        sin_in = sin_in * weight
        here = pl.ds(block * GROUP, GROUP)
        for o in range(FOLD // LANES):
            c = cos_out[:, o : o + 1]
            s = sin_out[:, o : o + 1]
            span = pl.ds(o * LANES, LANES)
            out_ref[0, 0, here, span] = (c * cos_in - s * sin_in).astype(jnp.bfloat16)
            out_ref[0, 1, here, span] = (-(s * cos_in + c * sin_in)).astype(jnp.bfloat16)


def phase_table(wave_order, groups, slots, offset, count):
    pairs = count // 2
    total = groups * pairs
    rows = 32
    return pl.pallas_call(
        functools.partial(table_kernel, pairs=pairs, slots=slots, offset=offset),
        out_shape=jax.ShapeDtypeStruct((2, 2, total, FOLD), jnp.bfloat16),
        grid_spec=pltpu.PrefetchScalarGridSpec(
            num_scalar_prefetch=2,
            grid=(2, total // rows),
            in_specs=[],
            out_specs=pl.BlockSpec((1, 2, rows, FOLD), lambda p, b, *_: (p, 0, b, 0)),
        ),
        compiler_params=pltpu.CompilerParams(vmem_limit_bytes=16 * MIB),
        cost_estimate=pl.CostEstimate(
            flops=16 * total * FOLD, bytes_accessed=8 * total * FOLD, transcendentals=0
        ),
        name="phases",
    )(jnp.zeros((1,), jnp.int32), wave_order)


def fourier_kernel(wave_ref, got_ref, table_ref, out_ref, left, held, *, levels):
    groups, shards, count, _ = got_ref.shape
    total = groups * count
    pairs = total // 2
    width = table_ref.shape[3]
    steps = FOLD // width
    step = pl.program_id(0)

    @pl.when(step == 0)
    def _():
        row = lax.broadcasted_iota(jnp.int32, (total, total), 0)
        column = lax.broadcasted_iota(jnp.int32, (total, total), 1)
        odd_row = (row >= pairs).astype(jnp.int32)
        chosen = (column // 2 == row - odd_row * pairs) & ((wave_ref[...] & 1) == odd_row)
        sort = chosen.astype(jnp.float32).astype(jnp.bfloat16)
        unit = (
            lax.broadcasted_iota(jnp.int32, (LANES, LANES), 0)
            == lax.broadcasted_iota(jnp.int32, (LANES, LANES), 1)
        ).astype(jnp.float32).astype(jnp.bfloat16)
        for shard in range(shards):
            mine = got_ref[:, shard].reshape(total, LANES)
            sorted_rows = jnp.dot(sort, mine, preferred_element_type=jnp.float32)
            turned = nt_dot(unit, sorted_rows.astype(jnp.bfloat16)).astype(jnp.bfloat16)
            for r in range(LANES // (2 * levels)):
                here = pl.ds(r * shards * levels + shard * levels, levels)
                for part in range(2):
                    at = (2 * r + part) * levels
                    for odd in range(2):
                        left[odd, here, pl.ds(part * pairs, pairs)] = turned[
                            at : at + levels, odd * pairs : (odd + 1) * pairs
                        ]

    @pl.when(step < steps)
    def _():
        sums = [
            jnp.dot(
                left[odd],
                table_ref[odd].reshape(2 * pairs, width),
                preferred_element_type=jnp.float32,
            )
            for odd in range(2)
        ]
        out_ref[...] = (sums[0] + sums[1]).astype(jnp.bfloat16)
        held[step] = (sums[0] - sums[1]).astype(jnp.bfloat16)

    @pl.when(step >= steps)
    def _():
        out_ref[...] = held[step - steps]


def fourier_sum(got, table, wave_order, levels):
    groups, shards, count, _ = got.shape
    total = groups * count
    rows = shards * LANES // 2
    width = 512
    steps = FOLD // width
    return pl.pallas_call(
        functools.partial(fourier_kernel, levels=levels),
        out_shape=jax.ShapeDtypeStruct((rows, NLON), jnp.bfloat16),
        grid_spec=pltpu.PrefetchScalarGridSpec(
            num_scalar_prefetch=0,
            grid=(2 * steps,),
            in_specs=[
                pl.BlockSpec((1, total), lambda x: (0, 0)),
                pl.BlockSpec(got.shape, lambda x: (0, 0, 0, 0)),
                pl.BlockSpec(
                    (2, 2, total // 2, width), lambda x: (0, 0, 0, jnp.minimum(x, steps - 1))
                ),
            ],
            out_specs=pl.BlockSpec((rows, width), lambda x: (0, x)),
            scratch_shapes=[
                pltpu.VMEM((2, rows, total), jnp.bfloat16),
                pltpu.VMEM((steps, rows, width), jnp.bfloat16),
            ],
        ),
        compiler_params=pltpu.CompilerParams(vmem_limit_bytes=48 * MIB),
        cost_estimate=pl.CostEstimate(
            flops=4 * rows * total * FOLD,
            bytes_accessed=4 * total * FOLD + 2 * rows * NLON,
            transcendentals=0,
        ),
        name="fourier",
    )(wave_order.reshape(1, total), got, table)


def local(spectra, polynomials, wave_order, row_cutoff):
    parts, levels, slots, degrees = spectra.shape
    groups = lax.axis_size("wave")
    shards = lax.axis_size("lev")
    targets = groups * shards
    basis = jnp.swapaxes(polynomials, 1, 2)
    sent = legendre(spectra, basis, wave_order, row_cutoff, 0, slots, targets)
    got = lax.all_to_all(sent, ("wave", "lev"), split_axis=0, concat_axis=0, tiled=True)
    table = phase_table(wave_order, groups, slots, 0, slots)
    grid = fourier_sum(got.reshape(groups, shards, slots, LANES), table, wave_order, levels)
    return grid.reshape(LANES // (parts * levels), shards * levels, NLON)


def solution(mesh):
    in_specs = (P(None, "lev", "wave", None), P("wave", None, None), P(), P())
    out_specs = P(("wave", "lev"), None, None)
    return jax.shard_map(local, mesh=mesh, in_specs=in_specs, out_specs=out_specs, check_vma=False)
```

time: 420 us -> 93.3 us (0.22)
  local copies, waits for them, and re-layouts: 196 us -> 11.4 us
  matrix products: 118 us -> 0 us
  Pallas kernels: 0 us -> 68.1 us
  blocking collectives: 64.1 us -> 0 us
  other arithmetic: 32.9 us -> 0 us
  waiting for transfers between devices: 0.01 us -> 5.59 us
    mul x7 -> x0, local copies, waits for them, and re-layouts: 182 us -> none  [make_phases(): table = weights * (with_cos * cos_first + with_sin * sin_first)]
    dot_general x3 -> x0, matrix products: 118 us -> none  [the longest x1 50.6 us: local(): jnp.einsum('ksvgq,skx->gqvx', shaped, phases, preferred_element_type=jnp....]
    pallas_call x0 -> x3, Pallas kernels: none -> 68.1 us  [the longest x1 28.6 us: legendre(): pl.pallas_call(legendre_kernel, out_shape=jax.ShapeDtypeStruct((targets,...]
    all_to_all x1 -> x0, blocking collectives: 64.1 us -> none  [local(): lax.all_to_all(longitudes, 'lev', split_axis=0, concat_axis=2, tiled=True)]
    mul x2 -> x0, other arithmetic: 25 us -> none  [the longest x1 25 us: local(): flipped = coeffs * parity_sign]
    unnamed x4 -> x12, local copies, waits for them, and re-layouts: 0.01 us -> 11.4 us
    all_to_all x3 -> x0, local copies, waits for them, and re-layouts: 7.11 us -> none  [the longest x2 5.45 us: local(): lax.all_to_all(fourier, 'wave', split_axis=3, concat_axis=0, tiled=True)]
    all_to_all x1, waiting for transfers between devices: 0.01 us -> 5.59 us  [local(): lax.all_to_all(sent, ('wave', 'lev'), split_axis=0, concat_axis=0, tiled=...]
  transfers between devices with their start and end apart: 1 -> 1, of which waited for: 0 -> 1; matrix products, arithmetic and copies ran while one was open for 45% -> 0% of each run, Pallas kernels for 0% -> 23%
where the time goes in v1:
time: 93.3 us; the launch traced here: 92.2 us
  Pallas kernels  68.1 us (73%)
  local copies, waits for them, and re-layouts  11.4 us (12%)
  starting transfers between devices  7.11 us (8%)
  waiting for transfers between devices  5.59 us (6%)
    pallas_call x1, Pallas kernels, legendre(): pl.pallas_call(legendre_kernel, out_shape=jax.ShapeDtypeStruct((targets,...  28.6 us
    pallas_call x1, Pallas kernels, phase_table(): pl.pallas_call(functools.partial(table_kernel, pairs=pairs, slots=slots,...  21.6 us
    pallas_call x1, Pallas kernels, fourier_sum(): pl.pallas_call(functools.partial(fourier_kernel, levels=levels), out_shap...  17.9 us
    unnamed x12, local copies, waits for them, and re-layouts  11.4 us
    all_to_all x1, starting transfers between devices, local(): lax.all_to_all(sent, ('wave', 'lev'), split_axis=0, concat_axis=0, tiled=...  7.11 us
    all_to_all x1, waiting for transfers between devices, local(): lax.all_to_all(sent, ('wave', 'lev'), split_axis=0, concat_axis=0, tiled=...  5.59 us
  transfers between devices with their start and end apart: 1, of which 1 were waited for; matrix products, arithmetic and copies ran while one was open for 0% of the time, Pallas kernels for 23%

profile of v1, /device:TPU:1, one launch (start us, length us, event | category | flops | bytes accessed | tf_op | source)
XLA Modules:
  0.0 92.2 jit_solution(16021806372126571013)
XLA Ops:
  0.0 0.0 copy-start.1
  0.0 0.7 copy-done.1
  0.7 0.0 copy-start.3
  0.7 4.7 %copy-done.3 = bf16[160,1280,32]{1,2,0:T(8,128)(2,1)S(1)} copy-done((bf16[160,1280,32]{1,2,0:T(8,128)(2,1)S(1)}, bf16[160,1280,32]{1,2,0:T(8,128)(2,1)}, u32[]{:S(2)}) %copy-start.3) | copy-done | bytes 13107224
  5.4 0.0 copy-start.4
  5.4 0.7 copy-done.4
  6.1 0.0 copy-start.5
  6.1 0.7 copy-done.5
  6.7 0.0 copy-start.2
  6.7 28.6 %legendre.1 = bf16[32,160,128]{2,1,0:T(8,128)(2,1)} custom-call(s32[2]{0:T(128)S(1)} %copy-done.5, s32[1280]{0:T(1024)S(1)} %copy-done.1, s32[64]{0:T(128)S(1)} %copy-done.4, bf16[2,32,160,1280]{3,2,1,0:T(8,128)(2,1)} %coeff_ref.1, bf16[160,32,1280]{2,1,0:T(8,128)(2,1)S(1)} %bitcast.4), custom_call_target="tpu_custom_call" | custom-call | flops 13421772800 | bytes 39321600 | tf_op jit(solution)/shard_map/legendre/pallas_call | solution.py:80
  35.3 7.1 %all-to-all-start = ((bf16[32,160,128]{2,1,0:T(8,128)(2,1)}), bf16[32,160,128]{2,1,0:T(8,128)(2,1)S(1)}, u32[]{:S(2)}, u32[]{:S(2)}) async-start(bf16[32,160,128]{2,1,0:T(8,128)(2,1)} %legendre.1), calls=%async_computation | async-start | bytes 2621440 | tf_op jit(solution)/shard_map/all_to_all | solution.py:272
  42.5 0.0 copy-done.2
  42.5 21.6 %phases.1.table_ref = bf16[2,2,640,2560]{3,2,1,0:T(8,128)(2,1)S(1)} custom-call(s32[1]{0:T(128)} %constant.1.clone.1.layout, s32[1280]{0:T(1024)S(1)} %copy-done.2), custom_call_target="tpu_custom_call" | custom-call | flops 26214400 | bytes 13107200 | tf_op jit(solution)/shard_map/phases/pallas_call | solution.py:163
  64.1 0.0 copy-start
  64.1 4.7 %copy-done = bf16[2,2,640,2560]{3,2,1,0:T(8,128)(2,1)} copy-done((bf16[2,2,640,2560]{3,2,1,0:T(8,128)(2,1)}, bf16[2,2,640,2560]{3,2,1,0:T(8,128)(2,1)S(1)}, u32[]{:S(2)}) %copy-start) | copy-done | bytes 13107224
  68.8 5.6 %all-to-all-done = bf16[32,160,128]{2,1,0:T(8,128)(2,1)S(1)} async-done(((bf16[32,160,128]{2,1,0:T(8,128)(2,1)}), bf16[32,160,128]{2,1,0:T(8,128)(2,1)S(1)}, u32[]{:S(2)}, u32[]{:S(2)}) %all-to-all-start) | async-done | bytes 1310752 | tf_op jit(solution)/shard_map/all_to_all | solution.py:272
  74.3 17.9 %fourier.1 = bf16[256,5120]{1,0:T(8,128)(2,1)} custom-call(s32[1,1280]{1,0:T(1,128)S(1)} %reshape.9.wave_ref, bf16[8,4,160,128]{3,2,1,0:T(8,128)(2,1)S(1)} %bitcast.3, bf16[2,2,640,2560]{3,2,1,0:T(8,128)(2,1)} %copy-done), custom_call_target="tpu_custom_call" | custom-call | flops 3355443200 | bytes 15728640 | tf_op jit(solution)/shard_map/fourier/pallas_call | solution.py:236
  (1 shorter events, 0.0 us)
Async XLA Ops:
  0.0 0.7 copy-start.1
  0.7 4.7 %copy-start.3 = (bf16[160,1280,32]{1,2,0:T(8,128)(2,1)S(1)}, bf16[160,1280,32]{1,2,0:T(8,128)(2,1)}, u32[]{:S(2)}) copy-start(bf16[160,1280,32]{1,2,0:T(8,128)(2,1)} %param.6) | copy-start | bytes 39321604
  5.4 0.7 copy-start.4
  6.1 0.7 copy-start.5
  6.7 35.7 %copy-start.2 = (s32[1280]{0:T(1024)S(1)}, s32[1280]{0:T(1024)}, u32[]{:S(2)}) copy-start(s32[1280]{0:T(1024)} %wave_ref.3) | copy-start | bytes 15364
  35.3 39.0 %all-to-all-start = ((bf16[32,160,128]{2,1,0:T(8,128)(2,1)}), bf16[32,160,128]{2,1,0:T(8,128)(2,1)S(1)}, u32[]{:S(2)}, u32[]{:S(2)}) async-start(bf16[32,160,128]{2,1,0:T(8,128)(2,1)} %legendre.1), calls=%async_computation | async-start | bytes 2621440 | tf_op jit(solution)/shard_map/all_to_all | solution.py:272
  64.1 4.7 %copy-start = (bf16[2,2,640,2560]{3,2,1,0:T(8,128)(2,1)}, bf16[2,2,640,2560]{3,2,1,0:T(8,128)(2,1)S(1)}, u32[]{:S(2)}) copy-start(bf16[2,2,640,2560]{3,2,1,0:T(8,128)(2,1)S(1)} %phases.1.table_ref) | copy-start | bytes 39321604

commit v2 on v0

v2 whole, which is shorter than its diff:
```python
import functools
import math

import jax
import jax.numpy as jnp
from jax import lax
from jax.experimental import pallas as pl
from jax.experimental.pallas import tpu as pltpu
from jax.sharding import PartitionSpec as P

NLON = 5120
FOLD = NLON // 2
LANES = 128
GROUP = 8
WIDTH = 256
VMEM_LIMIT = 60 * 1024 * 1024
DEPTH = 4


def nt_dot(left, right):
    return lax.dot_general(
        left, right, (((1,), (1,)), ((), ())), preferred_element_type=jnp.float32
    )


def one_hot(chosen):
    return chosen.astype(jnp.float32).astype(jnp.bfloat16)


def run_ahead(fetch, step, steps):
    @pl.when(step == 0)
    def _():
        for n in range(min(DEPTH - 1, steps)):
            for copy in fetch(n, n):
                copy.start()

    @pl.when(step + DEPTH - 1 < steps)
    def _():
        for copy in fetch(step + DEPTH - 1, lax.rem(step + DEPTH - 1, DEPTH)):
            copy.start()

    def wait():
        for copy in fetch(step, lax.rem(step, DEPTH)):
            copy.wait()

    return wait


def legendre_kernel(
    wave_ref,
    cut_ref,
    coeff_ref,
    basis_ref,
    out_ref,
    coeff_buffer,
    basis_buffer,
    low,
    high,
    sums,
    sort,
    limits,
    wide,
    tall,
    arrived,
    *,
    offset,
):
    parts, levels, slots, degrees = coeff_ref.shape
    half = basis_ref.shape[1]
    targets, count, _ = out_ref.shape
    batch = sums.shape[0]
    steps = count // GROUP
    pairs = GROUP // 2
    series = parts * levels
    columns = series * GROUP
    cut = low.shape[1]
    step = pl.program_id(0)
    slot = lax.axis_index("wave") * slots + offset + step * GROUP

    def fetch(at, buffer):
        here = pl.ds(pl.multiple_of(offset + at * GROUP, GROUP), GROUP)
        return [
            pltpu.make_async_copy(
                coeff_ref.at[:, :, here, :], coeff_buffer.at[buffer], arrived.at[0, buffer]
            ),
            pltpu.make_async_copy(
                basis_ref.at[here], basis_buffer.at[buffer], arrived.at[1, buffer]
            ),
        ]

    wait = run_ahead(fetch, step, steps)
    buffer = lax.rem(step, DEPTH)

    @pl.when(step == 0)
    def _():
        source = lax.broadcasted_iota(jnp.int32, (columns, columns), 0)
        target = lax.broadcasted_iota(jnp.int32, (columns, columns), 1)
        sort[...] = one_hot(
            (source // GROUP == target % series) & (source % GROUP == target // series)
        )
        for row in range(2 * half):
            limits[pl.ds(row, 1), :] = jnp.full((1, LANES), cut_ref[row], jnp.int32)

    wait()
    degree = lax.broadcasted_iota(jnp.int32, (1, degrees), 1)
    sign = (1 - 2 * (degree & 1)).astype(jnp.float32)
    waves = [wave_ref[slot + g] for g in range(GROUP)]
    longer = [(waves[2 * q] > waves[2 * q + 1]).astype(jnp.int32) for q in range(pairs)]

    def masked(wave, part, begin, end):
        usable = (degree[:, begin:end] <= degrees - 1 - wave).astype(jnp.float32)
        if part == 1:
            usable = usable * sign[:, begin:end]
        return usable.astype(jnp.bfloat16)

    for part in range(2):
        for g in range(GROUP):
            low[pl.ds((part * GROUP + g) * half, half), :] = basis_buffer[
                buffer, g, :, :cut
            ] * masked(waves[g], part, 0, cut)
        for q in range(pairs):
            wave = jnp.minimum(waves[2 * q], waves[2 * q + 1])
            high[pl.ds((part * pairs + q) * half, half), :] = basis_buffer[
                buffer, 2 * q + longer[q], :, cut:
            ] * masked(wave, part, cut, degrees)
    first = nt_dot(low[...], coeff_buffer[buffer, :, :, :, :cut].reshape(columns, cut))
    second = nt_dot(high[...], coeff_buffer[buffer, :, :, :, cut:].reshape(columns, degrees - cut))
    column_slot = lax.broadcasted_iota(jnp.int32, (1, columns), 1) % GROUP
    column_wave = jnp.zeros((1, columns), jnp.int32)
    column_swap = jnp.zeros((1, columns), jnp.int32)
    for g in range(GROUP):
        column_wave = jnp.where(column_slot == g, waves[g], column_wave)
        column_swap = jnp.where(column_slot == g, waves[g // 2 * 2] & 1, column_swap)
    swapped = [(column_swap == 1) & (column_slot % 2 == n) for n in range(2)]
    for part in range(2):
        total = jnp.zeros((half, columns), jnp.float32)
        for q in range(pairs):
            at = (part * pairs + q) * half
            total = jnp.where(column_slot == 2 * q + longer[q], second[at : at + half, :], total)
        for g in range(GROUP):
            at = (part * GROUP + g) * half
            total = total + jnp.where(column_slot == g, first[at : at + half, :], 0.0)
        for tile in range(columns // LANES):
            span = slice(tile * LANES, (tile + 1) * LANES)
            keep = column_wave[:, span] < limits[pl.ds(part * half, half), :]
            kept = jnp.where(keep, total[:, span], 0.0)
            even_first = jnp.where(
                swapped[0][:, span],
                pltpu.roll(kept, LANES - 1, 1),
                jnp.where(swapped[1][:, span], pltpu.roll(kept, 1, 1), kept),
            )
            sums[lax.rem(step, batch), pl.ds(part * half, half), span] = even_first.astype(
                jnp.bfloat16
            )

    @pl.when(lax.rem(step, batch) == batch - 1)
    def _():
        in_order = jnp.dot(
            sums[...].reshape(batch * 2 * half, columns),
            sort[...],
            preferred_element_type=jnp.float32,
        )
        for tile in range(columns // LANES):
            wide[tile] = in_order[:, tile * LANES : (tile + 1) * LANES]
        lane = lax.broadcasted_iota(jnp.int32, (targets, LANES), 1)
        for b in range(batch):
            first_pair = (step - (batch - 1) + b) * pairs
            for q in range(pairs):
                even = wide[q, pl.ds(b * 2 * half, targets, stride=2), :]
                odd = wide[q, pl.ds(b * 2 * half + 1, targets, stride=2), :]
                tall[pl.ds(first_pair + q, targets, stride=count), :] = jnp.where(
                    lane < series, even, pltpu.roll(odd, series, 1)
                )
                tall[pl.ds(count // 2 + first_pair + q, targets, stride=count), :] = jnp.where(
                    lane < series, pltpu.roll(even, series, 1), odd
                )

    @pl.when(step == steps - 1)
    def _():
        out_ref[...] = tall[...].reshape(out_ref.shape).astype(jnp.bfloat16)


def legendre(spectra, basis, wave_order, row_cutoff, offset, count, targets):
    parts, levels, slots, degrees = spectra.shape
    half = basis.shape[1]
    columns = parts * levels * GROUP
    cut = -(-degrees // 2 // 256) * 256
    steps = count // GROUP
    batch = max(n for n in range(1, 6) if steps % n == 0)
    anywhere = pl.BlockSpec(memory_space=pl.ANY)
    return pl.pallas_call(
        functools.partial(legendre_kernel, offset=offset),
        out_shape=jax.ShapeDtypeStruct((targets, count, LANES), jnp.bfloat16),
        grid_spec=pltpu.PrefetchScalarGridSpec(
            num_scalar_prefetch=2,
            grid=(steps,),
            in_specs=[anywhere, anywhere],
            out_specs=pl.BlockSpec((targets, count, LANES), lambda g, *_: (0, 0, 0)),
            scratch_shapes=[
                pltpu.VMEM((DEPTH, parts, levels, GROUP, degrees), jnp.bfloat16),
                pltpu.VMEM((DEPTH, GROUP, half, degrees), jnp.bfloat16),
                pltpu.VMEM((2 * GROUP * half, cut), jnp.bfloat16),
                pltpu.VMEM((GROUP * half, degrees - cut), jnp.bfloat16),
                pltpu.VMEM((batch, 2 * half, columns), jnp.bfloat16),
                pltpu.VMEM((columns, columns), jnp.bfloat16),
                pltpu.VMEM((2 * half, LANES), jnp.int32),
                pltpu.VMEM((columns // LANES, batch * 2 * half, LANES), jnp.float32),
                pltpu.VMEM((targets * count, LANES), jnp.float32),
                pltpu.SemaphoreType.DMA((2, DEPTH)),
            ],
        ),
        compiler_params=pltpu.CompilerParams(vmem_limit_bytes=VMEM_LIMIT),
        cost_estimate=pl.CostEstimate(
            flops=4 * count * half * degrees * columns,
            bytes_accessed=2 * count * degrees * (parts * levels + half),
            transcendentals=0,
        ),
        name="legendre",
    )(wave_order, row_cutoff, spectra, basis)


def cos_sin(steps):
    turns = jnp.floor(steps * (1.0 / NLON))
    residue = steps - turns * NLON
    quadrant = jnp.floor(residue * (4.0 / NLON) + 0.5)
    angle = (residue - quadrant * (NLON // 4)) * (2.0 * math.pi / NLON)
    square = angle * angle
    cosine = 1.0 + square * (
        -0.5 + square * (1.0 / 24 + square * (-1.0 / 720 + square * (1.0 / 40320)))
    )
    sine = angle * (
        1.0
        + square * (-1.0 / 6 + square * (1.0 / 120 + square * (-1.0 / 5040 + square / 362880.0)))
    )
    turn = quadrant.astype(jnp.int32)
    odd = (turn & 1) == 1
    flip_cos = ((turn + 1) & 2) == 2
    flip_sin = (turn & 2) == 2
    first = jnp.where(odd, sine, cosine)
    second = jnp.where(odd, cosine, sine)
    return jnp.where(flip_cos, -first, first), jnp.where(flip_sin, -second, second)


def table_kernel(wave_ref, out_ref, *, stride, count):
    blocks, _, _, _, rows, width = out_ref.shape
    odd_part = pl.program_id(0)
    top = wave_ref.shape[0] - 1
    pairs = min(rows, count // 2)
    sublane = lax.broadcasted_iota(jnp.int32, (GROUP, LANES), 0)
    lane = lax.broadcasted_iota(jnp.int32, (pairs, LANES), 1).astype(jnp.float32)

    @pl.loop(0, rows // pairs)
    def _(at):
        start = (pl.program_id(2) * (rows // pairs) + at) * stride + pl.program_id(1) * count
        waves = []
        for block in range(pairs // GROUP):
            column = jnp.zeros((GROUP, LANES), jnp.int32)
            for g in range(GROUP):
                column = jnp.where(sublane == g, wave_ref[start + 2 * (block * GROUP + g)], column)
            waves.append(column)
        column = jnp.concatenate(waves, axis=0)
        column = jnp.where((column & 1) == odd_part, column, top - column)
        wide = column.astype(jnp.float32)
        weight = jnp.where(column == 0, 1.0, 2.0)
        cosine, sine = cos_sin(wide * lane)
        turn_cos, turn_sin = cos_sin(wide * float(LANES))
        cosine = cosine * weight
        sine = sine * -weight
        here = pl.ds(pl.multiple_of(at * pairs, GROUP), pairs)
        for block in range(blocks):
            for o in range(width // LANES):
                if block + o > 0:
                    cosine, sine = (
                        cosine * turn_cos + sine * turn_sin,
                        sine * turn_cos - cosine * turn_sin,
                    )
                span = pl.ds(o * LANES, LANES)
                out_ref[block, 0, 0, 0, here, span] = cosine.astype(jnp.bfloat16)
                out_ref[block, 0, 0, 1, here, span] = sine.astype(jnp.bfloat16)


def phase_table(wave_order, groups, slots, chunks):
    count = slots // chunks
    total = groups * count // 2
    if chunks == 1:
        rows, stride, count = 64, 128, 128
    else:
        rows, stride = total // 2, slots
    shape = (FOLD // WIDTH, 2, chunks, 2, total, WIDTH)
    return pl.pallas_call(
        functools.partial(table_kernel, stride=stride, count=count),
        out_shape=jax.ShapeDtypeStruct(shape, jnp.bfloat16),
        grid_spec=pltpu.PrefetchScalarGridSpec(
            num_scalar_prefetch=1,
            grid=(2, chunks, total // rows),
            in_specs=[],
            out_specs=pl.BlockSpec(
                (FOLD // WIDTH, 1, 1, 2, rows, WIDTH), lambda p, c, b, *_: (0, p, c, 0, b, 0)
            ),
        ),
        compiler_params=pltpu.CompilerParams(vmem_limit_bytes=VMEM_LIMIT),
        cost_estimate=pl.CostEstimate(
            flops=16 * chunks * total * FOLD,
            bytes_accessed=8 * chunks * total * FOLD,
            transcendentals=0,
        ),
        name="phases",
    )(wave_order)


def arrange(got_ref, left, levels, begin):
    groups, shards, _, pairs, _ = got_ref.shape
    total = groups * pairs
    unit = one_hot(
        lax.broadcasted_iota(jnp.int32, (LANES, LANES), 0)
        == lax.broadcasted_iota(jnp.int32, (LANES, LANES), 1)
    )
    for odd in range(2):
        for shard in range(shards):
            block = got_ref[:, shard, odd].reshape(total, LANES)
            turned = nt_dot(unit, block).astype(jnp.bfloat16)
            for r in range(LANES // (2 * levels)):
                here = pl.ds((r * shards + shard) * levels, levels)
                for part in range(2):
                    at = (2 * r + part) * levels
                    left[odd, here, pl.ds(begin + part * total, total)] = turned[
                        at : at + levels, :
                    ]


def arrange_kernel(got_ref, out_ref, *, levels):
    arrange(got_ref, out_ref, levels, 0)


def arranged(got, levels):
    groups, shards, _, pairs, _ = got.shape
    total = groups * pairs
    rows = shards * LANES // 2
    return pl.pallas_call(
        functools.partial(arrange_kernel, levels=levels),
        out_shape=jax.ShapeDtypeStruct((2, rows, 2 * total), jnp.bfloat16),
        compiler_params=pltpu.CompilerParams(vmem_limit_bytes=VMEM_LIMIT),
        cost_estimate=pl.CostEstimate(
            flops=8 * total * rows * LANES, bytes_accessed=16 * total * rows, transcendentals=0
        ),
        name="arrange",
    )(got)


def fourier_kernel(*refs, levels, chunks):
    early_refs = refs[: chunks - 1]
    got_ref, table_ref, out_ref, table, left, held, arrived, done = refs[chunks - 1 :]
    steps, _, _, _, total, width = table_ref.shape
    span = 2 * total
    step = pl.program_id(0)
    slot = lax.rem(step, 2)

    def fetch(at, buffer):
        return [pltpu.make_async_copy(table_ref.at[at], table.at[buffer], arrived.at[buffer])]

    def copies(at, buffer):
        return [
            pltpu.make_async_copy(
                held.at[buffer, side],
                out_ref.at[:, pl.ds(pl.multiple_of(side * FOLD + at * width, width), width)],
                done.at[buffer, side],
            )
            for side in range(2)
        ]

    wait = run_ahead(fetch, step, steps)

    @pl.when(step == 0)
    def _():
        for chunk, early_ref in enumerate(early_refs):
            left[:, :, pl.ds(chunk * span, span)] = early_ref[...]
        arrange(got_ref, left, levels, (chunks - 1) * span)

    @pl.when(step >= 2)
    def _():
        for copy in copies(step - 2, slot):
            copy.wait()

    wait()
    sums = [
        jnp.dot(
            left[odd],
            table[lax.rem(step, DEPTH), odd].reshape(chunks * span, width),
            preferred_element_type=jnp.float32,
        )
        for odd in range(2)
    ]
    held[slot, 0] = (sums[0] + sums[1]).astype(jnp.bfloat16)
    held[slot, 1] = (sums[0] - sums[1]).astype(jnp.bfloat16)
    for copy in copies(step, slot):
        copy.start()

    @pl.when(step == steps - 1)
    def _():
        for copy in copies(step - 1, 1 - slot) + copies(step, slot):
            copy.wait()


def fourier_sum(early, got, table, levels):
    chunks = len(early) + 1
    groups, shards, _, pairs, _ = got.shape
    total = groups * pairs
    rows = shards * LANES // 2
    whole = pl.BlockSpec(memory_space=pltpu.VMEM)
    anywhere = pl.BlockSpec(memory_space=pl.ANY)
    return pl.pallas_call(
        functools.partial(fourier_kernel, levels=levels, chunks=chunks),
        out_shape=jax.ShapeDtypeStruct((rows, NLON), jnp.bfloat16),
        grid_spec=pltpu.PrefetchScalarGridSpec(
            num_scalar_prefetch=0,
            grid=(FOLD // WIDTH,),
            in_specs=[whole] * chunks + [anywhere],
            out_specs=anywhere,
            scratch_shapes=[
                pltpu.VMEM((DEPTH, *table.shape[1:]), jnp.bfloat16),
                pltpu.VMEM((2, rows, 2 * chunks * total), jnp.bfloat16),
                pltpu.VMEM((2, 2, rows, WIDTH), jnp.bfloat16),
                pltpu.SemaphoreType.DMA((DEPTH,)),
                pltpu.SemaphoreType.DMA((2, 2)),
            ],
        ),
        compiler_params=pltpu.CompilerParams(vmem_limit_bytes=VMEM_LIMIT),
        cost_estimate=pl.CostEstimate(
            flops=8 * rows * chunks * total * FOLD,
            bytes_accessed=8 * chunks * total * FOLD + 2 * rows * NLON,
            transcendentals=0,
        ),
        name="fourier",
    )(*early, got, table)


def local(spectra, polynomials, wave_order, row_cutoff):
    parts, levels, slots, degrees = spectra.shape
    groups = lax.axis_size("wave")
    shards = lax.axis_size("lev")
    basis = jnp.swapaxes(polynomials, 1, 2)
    chunks = 2 if slots % (4 * GROUP) == 0 else 1
    count = slots // chunks
    got = []
    for chunk in range(chunks):
        sent = legendre(
            spectra, basis, wave_order, row_cutoff, chunk * count, count, groups * shards
        )
        arrived = lax.all_to_all(sent, ("wave", "lev"), split_axis=0, concat_axis=0, tiled=True)
        got.append(arrived.reshape(groups, shards, 2, count // 2, LANES))
    table = phase_table(wave_order, groups, slots, chunks)
    early = [arranged(one, levels) for one in got[:-1]]
    grid = fourier_sum(early, got[-1], table, levels)
    return grid.reshape(LANES // (parts * levels), shards * levels, NLON)


def solution(mesh):
    in_specs = (P(None, "lev", "wave", None), P("wave", None, None), P(), P())
    out_specs = P(("wave", "lev"), None, None)
    return jax.shard_map(local, mesh=mesh, in_specs=in_specs, out_specs=out_specs, check_vma=False)
```

time: 420 us -> 70.2 us (0.17)
  local copies, waits for them, and re-layouts: 196 us -> 0.86 us
  matrix products: 118 us -> 0 us
  blocking collectives: 64.1 us -> 0 us
  Pallas kernels: 0 us -> 47.7 us
  other arithmetic: 32.9 us -> 0 us
  waiting for transfers between devices: 0.01 us -> 10.9 us
  starting transfers between devices: 5.22 us -> 10.2 us
    mul x7 -> x0, local copies, waits for them, and re-layouts: 182 us -> none  [make_phases(): table = weights * (with_cos * cos_first + with_sin * sin_first)]
    dot_general x3 -> x0, matrix products: 118 us -> none  [the longest x1 50.6 us: local(): jnp.einsum('ksvgq,skx->gqvx', shaped, phases, preferred_element_type=jnp....]
    all_to_all x1 -> x0, blocking collectives: 64.1 us -> none  [local(): lax.all_to_all(longitudes, 'lev', split_axis=0, concat_axis=2, tiled=True)]
    pallas_call x0 -> x5, Pallas kernels: none -> 47.7 us  [the longest x2 26.5 us: legendre(): pl.pallas_call(functools.partial(legendre_kernel, offset=offset), out_sha...]
    mul x2 -> x0, other arithmetic: 25 us -> none  [the longest x1 25 us: local(): flipped = coeffs * parity_sign]
    all_to_all x1 -> x2, waiting for transfers between devices: 0.01 us -> 10.9 us  [local(): lax.all_to_all(sent, ('wave', 'lev'), split_axis=0, concat_axis=0, tiled=...]
    all_to_all x3 -> x0, local copies, waits for them, and re-layouts: 7.11 us -> none  [the longest x2 5.45 us: local(): lax.all_to_all(fourier, 'wave', split_axis=3, concat_axis=0, tiled=True)]
    concatenate x1 -> x0, local copies, waits for them, and re-layouts: 5.28 us -> none  [local(): fourier = jnp.concatenate([northern, southern], axis=3).astype(jnp.bfloat16)]
  transfers between devices with their start and end apart: 1 -> 2, of which waited for: 0 -> 2; matrix products, arithmetic and copies ran while one was open for 45% -> 0% of each run, Pallas kernels for 0% -> 36%
where the time goes in v2:
time: 70.2 us; the launch traced here: 69.7 us
  Pallas kernels  47.7 us (68%)
  waiting for transfers between devices  10.9 us (16%)
  starting transfers between devices  10.2 us (15%)
  local copies, waits for them, and re-layouts  0.86 us (1%)
    pallas_call x2, Pallas kernels, legendre(): pl.pallas_call(functools.partial(legendre_kernel, offset=offset), out_sha...  26.5 us
    all_to_all x2, waiting for transfers between devices, local(): lax.all_to_all(sent, ('wave', 'lev'), split_axis=0, concat_axis=0, tiled=...  10.9 us
    all_to_all x2, starting transfers between devices, local(): lax.all_to_all(sent, ('wave', 'lev'), split_axis=0, concat_axis=0, tiled=...  10.2 us
    pallas_call x1, Pallas kernels, phase_table(): pl.pallas_call(functools.partial(table_kernel, stride=stride, count=count...  9.44 us
    pallas_call x1, Pallas kernels, fourier_sum(): pl.pallas_call(functools.partial(fourier_kernel, levels=levels, chunks=ch...  9.24 us
    pallas_call x1, Pallas kernels, arranged(): pl.pallas_call(functools.partial(arrange_kernel, levels=levels), out_shap...  2.45 us
  transfers between devices with their start and end apart: 2, of which 2 were waited for; matrix products, arithmetic and copies ran while one was open for 0% of the time, Pallas kernels for 36%

profile of v2, /device:TPU:1, one launch (start us, length us, event | category | flops | bytes accessed | tf_op | source)
XLA Modules:
  0.0 69.7 jit_solution(2848955389147960891)
XLA Ops:
  0.0 13.2 %legendre.2 = bf16[32,80,128]{2,1,0:T(8,128)(2,1)} custom-call(s32[1280]{0:T(1024)} %wave_ref.5, s32[64]{0:T(128)} %cut_ref.3, bf16[2,32,160,1280]{3,2,1,0:T(8,128)(2,1)} %coeff_ref.3, bf16[160,32,1280]{2,1,0:T(8,128)(2,1)} %bitcast.4), custom_call_target="tpu_custom_call" | custom-call | flops 6710886400 | bytes 19660800 | tf_op jit(solution)/shard_map/legendre/pallas_call | solution.py:191
  13.3 7.1 %all-to-all-start = ((bf16[32,80,128]{2,1,0:T(8,128)(2,1)}), bf16[32,80,128]{2,1,0:T(8,128)(2,1)S(1)}, u32[]{:S(2)}, u32[]{:S(2)}) async-start(bf16[32,80,128]{2,1,0:T(8,128)(2,1)} %legendre.2), calls=%async_computation | async-start | bytes 1310720 | tf_op jit(solution)/shard_map/all_to_all | solution.py:449
  20.4 13.3 %legendre.3 = bf16[32,80,128]{2,1,0:T(8,128)(2,1)} custom-call(s32[1280]{0:T(1024)} %wave_ref.5, s32[64]{0:T(128)} %cut_ref.3, bf16[2,32,160,1280]{3,2,1,0:T(8,128)(2,1)} %coeff_ref.3, bf16[160,32,1280]{2,1,0:T(8,128)(2,1)} %bitcast.5), custom_call_target="tpu_custom_call" | custom-call | flops 6710886400 | bytes 19660800 | tf_op jit(solution)/shard_map/legendre/pallas_call | solution.py:191
  33.6 4.8 %all-to-all-done = bf16[32,80,128]{2,1,0:T(8,128)(2,1)S(1)} async-done(((bf16[32,80,128]{2,1,0:T(8,128)(2,1)}), bf16[32,80,128]{2,1,0:T(8,128)(2,1)S(1)}, u32[]{:S(2)}, u32[]{:S(2)}) %all-to-all-start) | async-done | bytes 655392 | tf_op jit(solution)/shard_map/all_to_all | solution.py:449
  38.4 0.0 copy-start.1
  38.4 3.2 %all-to-all-start.1 = ((bf16[32,80,128]{2,1,0:T(8,128)(2,1)}), bf16[32,80,128]{2,1,0:T(8,128)(2,1)S(1)}, u32[]{:S(2)}, u32[]{:S(2)}) async-start(bf16[32,80,128]{2,1,0:T(8,128)(2,1)} %legendre.3), calls=%async_computation.1 | async-start | bytes 1310720 | tf_op jit(solution)/shard_map/all_to_all | solution.py:449
  41.6 9.4 %phases.1.refs_2_ = bf16[10,2,2,2,320,256]{5,4,3,2,1,0:T(8,128)(2,1)} custom-call(s32[1280]{0:T(1024)} %wave_ref.5), custom_call_target="tpu_custom_call" | custom-call | flops 26214400 | bytes 13107200 | tf_op jit(solution)/shard_map/phases/pallas_call | solution.py:290
  51.0 0.0 copy-done.1
  51.0 2.4 %arrange.1.refs_0_ = bf16[2,256,640]{2,1,0:T(8,128)(2,1)} custom-call(bf16[8,4,2,40,128]{4,3,2,1,0:T(8,128)(2,1)} %bitcast.7), custom_call_target="tpu_custom_call" | custom-call | flops 83886080 | bytes 1310720 | tf_op jit(solution)/shard_map/arrange/pallas_call | solution.py:339
  53.5 6.2 %all-to-all-done.1 = bf16[32,80,128]{2,1,0:T(8,128)(2,1)S(1)} async-done(((bf16[32,80,128]{2,1,0:T(8,128)(2,1)}), bf16[32,80,128]{2,1,0:T(8,128)(2,1)S(1)}, u32[]{:S(2)}, u32[]{:S(2)}) %all-to-all-start.1) | async-done | bytes 655392 | tf_op jit(solution)/shard_map/all_to_all | solution.py:449
  59.6 0.0 copy-start
  59.6 0.9 %copy-done = bf16[32,80,128]{2,1,0:T(8,128)(2,1)} copy-done((bf16[32,80,128]{2,1,0:T(8,128)(2,1)}, bf16[32,80,128]{2,1,0:T(8,128)(2,1)S(1)}, u32[]{:S(2)}) %copy-start) | copy-done | bytes 655384
  60.5 9.2 %fourier.1 = bf16[256,5120]{1,0:T(8,128)(2,1)} custom-call(bf16[2,256,640]{2,1,0:T(8,128)(2,1)} %arrange.1.refs_0_, bf16[8,4,2,40,128]{4,3,2,1,0:T(8,128)(2,1)} %bitcast.6, bf16[10,2,2,2,320,256]{5,4,3,2,1,0:T(8,128)(2,1)} %phases.1.refs_2_), custom_call_target="tpu_custom_call" | custom-call | flops 3355443200 | bytes 15728640 | tf_op jit(solution)/shard_map/fourier/pallas_call | solution.py:411
Async XLA Ops:
  13.3 25.2 %all-to-all-start = ((bf16[32,80,128]{2,1,0:T(8,128)(2,1)}), bf16[32,80,128]{2,1,0:T(8,128)(2,1)S(1)}, u32[]{:S(2)}, u32[]{:S(2)}) async-start(bf16[32,80,128]{2,1,0:T(8,128)(2,1)} %legendre.2), calls=%async_computation | async-start | bytes 1310720 | tf_op jit(solution)/shard_map/all_to_all | solution.py:449
  38.4 12.6 %copy-start.1 = (bf16[32,80,128]{2,1,0:T(8,128)(2,1)}, bf16[32,80,128]{2,1,0:T(8,128)(2,1)S(1)}, u32[]{:S(2)}) copy-start(bf16[32,80,128]{2,1,0:T(8,128)(2,1)S(1)} %all-to-all-done) | copy-start | bytes 1966084
  38.4 21.2 %all-to-all-start.1 = ((bf16[32,80,128]{2,1,0:T(8,128)(2,1)}), bf16[32,80,128]{2,1,0:T(8,128)(2,1)S(1)}, u32[]{:S(2)}, u32[]{:S(2)}) async-start(bf16[32,80,128]{2,1,0:T(8,128)(2,1)} %legendre.3), calls=%async_computation.1 | async-start | bytes 1310720 | tf_op jit(solution)/shard_map/all_to_all | solution.py:449
  59.6 0.9 %copy-start = (bf16[32,80,128]{2,1,0:T(8,128)(2,1)}, bf16[32,80,128]{2,1,0:T(8,128)(2,1)S(1)}, u32[]{:S(2)}) copy-start(bf16[32,80,128]{2,1,0:T(8,128)(2,1)S(1)} %all-to-all-done.1) | copy-start | bytes 1966084

commit v3 on v2

v3 whole, which is shorter than its diff:
```python
import functools
import math

import jax
import jax.numpy as jnp
from jax import lax
from jax.experimental import pallas as pl
from jax.experimental.pallas import tpu as pltpu
from jax.sharding import PartitionSpec as P

NLON = 5120
FOLD = NLON // 4
LANES = 128
GROUP = 8
WIDTH = 256
VMEM_LIMIT = 60 * 1024 * 1024
DEPTH = 3
ROOM = 24


def nt_dot(left, right):
    return lax.dot_general(
        left, right, (((1,), (1,)), ((), ())), preferred_element_type=jnp.float32
    )


def one_hot(chosen):
    return chosen.astype(jnp.float32).astype(jnp.bfloat16)


def run_ahead(fetch, step, steps):
    @pl.when(step == 0)
    def _():
        for n in range(min(DEPTH - 1, steps)):
            for copy in fetch(n, n):
                copy.start()

    @pl.when(step + DEPTH - 1 < steps)
    def _():
        for copy in fetch(step + DEPTH - 1, lax.rem(step + DEPTH - 1, DEPTH)):
            copy.start()

    def wait():
        for copy in fetch(step, lax.rem(step, DEPTH)):
            copy.wait()

    return wait


def legendre_kernel(
    wave_ref,
    cut_ref,
    coeff_ref,
    basis_ref,
    out_ref,
    coeff_buffer,
    basis_buffer,
    low,
    high,
    sums,
    sort,
    limits,
    wide,
    tall,
    arrived,
    *,
    offset,
):
    parts, levels, slots, degrees = coeff_ref.shape
    half = basis_ref.shape[1]
    targets, count, _ = out_ref.shape
    batch = sums.shape[0]
    steps = count // (GROUP * batch)
    pairs = GROUP // 2
    series = parts * levels
    columns = series * GROUP
    cut = low.shape[2]
    step = pl.program_id(0)
    slot = lax.axis_index("wave") * slots + offset + step * batch * GROUP

    def fetch(at, buffer):
        copies = []
        for b in range(batch):
            first = pl.multiple_of(offset + (at * batch + b) * GROUP, GROUP)
            here = pl.ds(first, GROUP)
            copies += [
                pltpu.make_async_copy(
                    coeff_ref.at[:, :, here, :],
                    coeff_buffer.at[buffer, b],
                    arrived.at[0, buffer, b],
                ),
                pltpu.make_async_copy(
                    basis_ref.at[here], basis_buffer.at[buffer, b], arrived.at[1, buffer, b]
                ),
            ]
        return copies

    wait = run_ahead(fetch, step, steps)
    buffer = lax.rem(step, DEPTH)

    @pl.when(step == 0)
    def _():
        source = lax.broadcasted_iota(jnp.int32, (columns, columns), 0)
        target = lax.broadcasted_iota(jnp.int32, (columns, columns), 1)
        sort[...] = one_hot(
            (source // GROUP == target % series) & (source % GROUP == target // series)
        )
        for row in range(2 * half):
            limits[pl.ds(row, 1), :] = jnp.full((1, LANES), cut_ref[row], jnp.int32)

    def spread(at):
        in_order = jnp.dot(
            sums[...].reshape(batch * 2 * half, columns),
            sort[...],
            preferred_element_type=jnp.float32,
        )
        for tile in range(columns // LANES):
            wide[tile] = in_order[:, tile * LANES : (tile + 1) * LANES]
        lane = lax.broadcasted_iota(jnp.int32, (targets, LANES), 1)
        for b in range(batch):
            first_pair = (at * batch + b) * pairs
            for q in range(pairs):
                even = wide[q, pl.ds(b * 2 * half, targets, stride=2), :]
                odd = wide[q, pl.ds(b * 2 * half + 1, targets, stride=2), :]
                tall[pl.ds(first_pair + q, targets, stride=count), :] = jnp.where(
                    lane < series, even, pltpu.roll(odd, series, 1)
                )
                tall[pl.ds(count // 2 + first_pair + q, targets, stride=count), :] = jnp.where(
                    lane < series, pltpu.roll(even, series, 1), odd
                )

    wait()
    spread(jnp.maximum(step - 1, 0))
    degree = lax.broadcasted_iota(jnp.int32, (1, degrees), 1)
    sign = (1 - 2 * (degree & 1)).astype(jnp.float32)

    def masked(wave, part, begin, end):
        usable = (degree[:, begin:end] <= degrees - 1 - wave).astype(jnp.float32)
        if part == 1:
            usable = usable * sign[:, begin:end]
        return usable.astype(jnp.bfloat16)

    waves = [[wave_ref[slot + b * GROUP + g] for g in range(GROUP)] for b in range(batch)]
    longer = [
        [(waves[b][2 * q] > waves[b][2 * q + 1]).astype(jnp.int32) for q in range(pairs)]
        for b in range(batch)
    ]
    for b in range(batch):
        for part in range(2):
            for g in range(GROUP):
                low[b, pl.ds((part * GROUP + g) * half, half), :] = basis_buffer[
                    buffer, b, g, :, :cut
                ] * masked(waves[b][g], part, 0, cut)
            for q in range(pairs):
                wave = jnp.minimum(waves[b][2 * q], waves[b][2 * q + 1])
                high[b, pl.ds((part * pairs + q) * half, half), :] = basis_buffer[
                    buffer, b, 2 * q + longer[b][q], :, cut:
                ] * masked(wave, part, cut, degrees)
    column_slot = lax.broadcasted_iota(jnp.int32, (1, columns), 1) % GROUP
    for b in range(batch):
        first = nt_dot(low[b], coeff_buffer[buffer, b, :, :, :, :cut].reshape(columns, cut))
        second = nt_dot(
            high[b], coeff_buffer[buffer, b, :, :, :, cut:].reshape(columns, degrees - cut)
        )
        column_wave = jnp.zeros((1, columns), jnp.int32)
        column_swap = jnp.zeros((1, columns), jnp.int32)
        for g in range(GROUP):
            column_wave = jnp.where(column_slot == g, waves[b][g], column_wave)
            column_swap = jnp.where(column_slot == g, waves[b][g // 2 * 2] & 1, column_swap)
        swapped = [(column_swap == 1) & (column_slot % 2 == n) for n in range(2)]
        for part in range(2):
            total = jnp.zeros((half, columns), jnp.float32)
            for q in range(pairs):
                at = (part * pairs + q) * half
                total = jnp.where(
                    column_slot == 2 * q + longer[b][q], second[at : at + half, :], total
                )
            own = jnp.zeros((half, columns), jnp.float32)
            for g in range(GROUP):
                at = (part * GROUP + g) * half
                own = jnp.where(column_slot == g, first[at : at + half, :], own)
            total = total + own
            for tile in range(columns // LANES):
                span = slice(tile * LANES, (tile + 1) * LANES)
                keep = column_wave[:, span] < limits[pl.ds(part * half, half), :]
                kept = jnp.where(keep, total[:, span], 0.0)
                even_first = jnp.where(
                    swapped[0][:, span],
                    pltpu.roll(kept, LANES - 1, 1),
                    jnp.where(swapped[1][:, span], pltpu.roll(kept, 1, 1), kept),
                )
                sums[b, pl.ds(part * half, half), span] = even_first.astype(jnp.bfloat16)

    @pl.when(step == steps - 1)
    def _():
        spread(step)
        out_ref[...] = tall[...].reshape(out_ref.shape).astype(jnp.bfloat16)


def legendre(spectra, basis, wave_order, row_cutoff, offset, count, targets):
    parts, levels, slots, degrees = spectra.shape
    half = basis.shape[1]
    columns = parts * levels * GROUP
    cut = -(-degrees // 2 // 256) * 256
    batch = 2 if count % (2 * GROUP) == 0 else 1
    steps = count // (batch * GROUP)
    anywhere = pl.BlockSpec(memory_space=pl.ANY)
    return pl.pallas_call(
        functools.partial(legendre_kernel, offset=offset),
        out_shape=jax.ShapeDtypeStruct((targets, count, LANES), jnp.bfloat16),
        grid_spec=pltpu.PrefetchScalarGridSpec(
            num_scalar_prefetch=2,
            grid=(steps,),
            in_specs=[anywhere, anywhere],
            out_specs=pl.BlockSpec((targets, count, LANES), lambda g, *_: (0, 0, 0)),
            scratch_shapes=[
                pltpu.VMEM((DEPTH, batch, parts, levels, GROUP, degrees), jnp.bfloat16),
                pltpu.VMEM((DEPTH, batch, GROUP, half, degrees), jnp.bfloat16),
                pltpu.VMEM((batch, 2 * GROUP * half, cut), jnp.bfloat16),
                pltpu.VMEM((batch, GROUP * half, degrees - cut), jnp.bfloat16),
                pltpu.VMEM((batch, 2 * half, columns), jnp.bfloat16),
                pltpu.VMEM((columns, columns), jnp.bfloat16),
                pltpu.VMEM((2 * half, LANES), jnp.int32),
                pltpu.VMEM((columns // LANES, batch * 2 * half, LANES), jnp.float32),
                pltpu.VMEM((targets * count, LANES), jnp.float32),
                pltpu.SemaphoreType.DMA((2, DEPTH, batch)),
            ],
        ),
        compiler_params=pltpu.CompilerParams(vmem_limit_bytes=VMEM_LIMIT),
        cost_estimate=pl.CostEstimate(
            flops=4 * count * half * degrees * columns,
            bytes_accessed=2 * count * degrees * (parts * levels + half),
            transcendentals=0,
        ),
        name="legendre",
    )(wave_order, row_cutoff, spectra, basis)


def cos_sin(steps):
    turns = jnp.floor(steps * (1.0 / NLON))
    residue = steps - turns * NLON
    quadrant = jnp.floor(residue * (4.0 / NLON) + 0.5)
    angle = (residue - quadrant * (NLON // 4)) * (2.0 * math.pi / NLON)
    square = angle * angle
    cosine = 1.0 + square * (
        -0.5 + square * (1.0 / 24 + square * (-1.0 / 720 + square * (1.0 / 40320)))
    )
    sine = angle * (
        1.0
        + square * (-1.0 / 6 + square * (1.0 / 120 + square * (-1.0 / 5040 + square / 362880.0)))
    )
    turn = quadrant.astype(jnp.int32)
    odd = (turn & 1) == 1
    flip_cos = ((turn + 1) & 2) == 2
    flip_sin = (turn & 2) == 2
    first = jnp.where(odd, sine, cosine)
    second = jnp.where(odd, cosine, sine)
    return jnp.where(flip_cos, -first, first), jnp.where(flip_sin, -second, second)


def table_kernel(wave_ref, out_ref, *, segments):
    odd_part = pl.program_id(0)
    top = wave_ref.shape[0] - 1
    sublane = lax.broadcasted_iota(jnp.int32, (GROUP, LANES), 0)
    begin = 0
    for groups, stride, first, pairs in segments:
        lane = lax.broadcasted_iota(jnp.int32, (pairs, LANES), 1).astype(jnp.float32)

        @pl.loop(0, groups)
        def _(group):
            waves = []
            for block in range(0, pairs, GROUP):
                column = jnp.zeros((GROUP, LANES), jnp.int32)
                for g in range(GROUP):
                    wave = wave_ref[group * stride + first + 2 * (block + g)]
                    column = jnp.where(sublane == g, wave, column)
                waves.append(column)
            column = jnp.concatenate(waves, axis=0)
            column = jnp.where((column & 1) == odd_part, column, top - column)
            wide = column.astype(jnp.float32)
            weight = jnp.where(column == 0, 1.0, 2.0)
            cosine, sine = cos_sin(wide * lane)
            turn_cos, turn_sin = cos_sin(wide * float(LANES))
            cosine = cosine * weight
            sine = sine * -weight
            here = pl.ds(pl.multiple_of(begin + group * pairs, GROUP), pairs)
            for tile in range(FOLD // LANES + 1):
                if tile > 0:
                    cosine, sine = (
                        cosine * turn_cos + sine * turn_sin,
                        sine * turn_cos - cosine * turn_sin,
                    )
                block, at = divmod(tile * LANES, WIDTH)
                out_ref[block, 0, 0, here, pl.ds(at, LANES)] = cosine.astype(jnp.bfloat16)
                out_ref[block, 0, 1, here, pl.ds(at, LANES)] = sine.astype(jnp.bfloat16)

        begin += groups * pairs


def phase_table(wave_order, slots, counts):
    waves = wave_order.shape[0]
    pairs = waves // 2
    if len(counts) == 1:
        segments = ((waves // 64, 64, 0, 32),)
    else:
        segments = tuple(
            (waves // slots, slots, sum(counts[:n]), count // 2) for n, count in enumerate(counts)
        )
    blocks = FOLD // WIDTH + 1
    return pl.pallas_call(
        functools.partial(table_kernel, segments=segments),
        out_shape=jax.ShapeDtypeStruct((blocks, 2, 2, pairs, WIDTH), jnp.bfloat16),
        grid_spec=pltpu.PrefetchScalarGridSpec(
            num_scalar_prefetch=1,
            grid=(2,),
            in_specs=[],
            out_specs=pl.BlockSpec(
                (blocks, 1, 2, pairs, WIDTH), lambda p, *_: (0, p, 0, 0, 0)
            ),
        ),
        compiler_params=pltpu.CompilerParams(vmem_limit_bytes=VMEM_LIMIT),
        cost_estimate=pl.CostEstimate(
            flops=16 * waves * FOLD, bytes_accessed=4 * waves * FOLD, transcendentals=0
        ),
        name="phases",
    )(wave_order)


def arrange(got_ref, left, levels, begin):
    groups, shards, _, pairs, _ = got_ref.shape
    total = groups * pairs
    unit = one_hot(
        lax.broadcasted_iota(jnp.int32, (LANES, LANES), 0)
        == lax.broadcasted_iota(jnp.int32, (LANES, LANES), 1)
    )
    for odd in range(2):
        for shard in range(shards):
            block = got_ref[:, shard, odd].reshape(total, LANES)
            turned = nt_dot(unit, block).astype(jnp.bfloat16)
            for r in range(LANES // (2 * levels)):
                here = pl.ds((r * shards + shard) * levels, levels)
                for part in range(2):
                    at = (2 * r + part) * levels
                    left[odd, part, here, pl.ds(begin, total)] = turned[at : at + levels, :]


def arrange_kernel(got_ref, out_ref, *, levels):
    arrange(got_ref, out_ref.at[0], levels, 0)


def arranged(got, levels):
    groups, shards, _, pairs, _ = got.shape
    total = groups * pairs
    rows = shards * LANES // 2
    return pl.pallas_call(
        functools.partial(arrange_kernel, levels=levels),
        out_shape=jax.ShapeDtypeStruct((ROOM, 2, 2, rows, total), jnp.bfloat16),
        grid=(1,),
        in_specs=[pl.BlockSpec(got.shape, lambda g: (0, 0, 0, 0, 0))],
        out_specs=pl.BlockSpec((1, 2, 2, rows, total), lambda g: (0, 0, 0, 0, 0)),
        compiler_params=pltpu.CompilerParams(vmem_limit_bytes=VMEM_LIMIT),
        cost_estimate=pl.CostEstimate(
            flops=8 * total * rows * LANES, bytes_accessed=16 * total * rows, transcendentals=0
        ),
        name="arrange",
    )(got)


def fourier_kernel(*refs, levels, early):
    early_refs = refs[:early]
    got_ref, table_ref, out_ref = refs[early : early + 3]
    got, table, edge, left, back, result, fetched, arrived, done = refs[early + 3 :]
    blocks = table_ref.shape[0] - 1
    moves = [pltpu.make_async_copy(got_ref, got, fetched.at[0])]
    edge_move = pltpu.make_async_copy(
        table_ref.at[blocks, :, :, :, pl.ds(0, LANES)], edge, fetched.at[1]
    )
    begin = 0
    for n, early_ref in enumerate(early_refs):
        span = early_ref.shape[4]
        target = left.at[:, :, :, pl.ds(begin, span)]
        moves.append(pltpu.make_async_copy(early_ref.at[0], target, fetched.at[n + 2]))
        begin += span
    order = list(range(blocks - 1, -1, -1))
    tables = {
        at: pltpu.make_async_copy(table_ref.at[at], table.at[at], arrived.at[at]) for at in order
    }
    for move in moves:
        move.start()
    for at in order:
        tables[at].start()
    edge_move.start()
    moves[0].wait()
    arrange(got, left, levels, begin)
    for move in moves[1:]:
        move.wait()

    def combine(block):
        sums = [
            [
                jnp.dot(left[odd, part], block[odd, part], preferred_element_type=jnp.float32)
                for part in range(2)
            ]
            for odd in range(2)
        ]
        return [
            (sums[0][part] + sums[1][part], sums[0][part] - sums[1][part]) for part in range(2)
        ]

    mirror = one_hot(
        lax.broadcasted_iota(jnp.int32, (2 * LANES, LANES), 0)
        == LANES - lax.broadcasted_iota(jnp.int32, (2 * LANES, LANES), 1)
    )
    stores = []

    def reverse(first, tile):
        for side in range(2):
            turned = jnp.dot(
                back[side, :, pl.ds(first + tile * LANES, 2 * LANES)],
                mirror,
                preferred_element_type=jnp.float32,
            )
            to = (2 * side + 2) * FOLD - first - (tile + 1) * LANES
            result[:, pl.ds(to, LANES)] = turned.astype(jnp.bfloat16)

    def store(at, n, start):
        span = pl.ds(start, WIDTH)
        copy = pltpu.make_async_copy(result.at[:, span], out_ref.at[:, span], done.at[at, n])
        copy.start()
        stores.append(copy)

    tiles = WIDTH // LANES
    for at in order:
        tables[at].wait()
        (a, c), (b, d) = combine(table.at[at])
        first = at * WIDTH
        result[:, pl.ds(first, WIDTH)] = (a + b).astype(jnp.bfloat16)
        result[:, pl.ds(2 * FOLD + first, WIDTH)] = (c + d).astype(jnp.bfloat16)
        back[0, :, pl.ds(first, WIDTH)] = (c - d).astype(jnp.bfloat16)
        back[1, :, pl.ds(first, WIDTH)] = (a - b).astype(jnp.bfloat16)
        store(at, 0, first)
        store(at, 1, 2 * FOLD + first)
        outermost = at == blocks - 1
        for tile in range(tiles - 1 if outermost else tiles):
            reverse(first, tile)
        if not outermost:
            store(at, 2, 2 * FOLD - first - WIDTH)
            store(at, 3, 4 * FOLD - first - WIDTH)
    edge_move.wait()
    (a, c), (b, d) = combine(edge)
    back[0, :, pl.ds(FOLD, LANES)] = (c - d).astype(jnp.bfloat16)
    back[1, :, pl.ds(FOLD, LANES)] = (a - b).astype(jnp.bfloat16)
    reverse(FOLD - WIDTH, tiles - 1)
    store(blocks - 1, 2, FOLD)
    store(blocks - 1, 3, 3 * FOLD)
    for copy in stores:
        copy.wait()


def fourier_sum(early, got, table, levels):
    shards = got.shape[1]
    rows = shards * LANES // 2
    blocks, _, _, pairs, _ = table.shape
    blocks -= 1
    anywhere = pl.BlockSpec(memory_space=pl.ANY)
    return pl.pallas_call(
        functools.partial(fourier_kernel, levels=levels, early=len(early)),
        out_shape=jax.ShapeDtypeStruct((rows, NLON), jnp.bfloat16),
        in_specs=[anywhere] * (len(early) + 2),
        out_specs=anywhere,
        scratch_shapes=[
            pltpu.VMEM(got.shape, jnp.bfloat16),
            pltpu.VMEM((blocks, *table.shape[1:]), jnp.bfloat16),
            pltpu.VMEM((2, 2, pairs, LANES), jnp.bfloat16),
            pltpu.VMEM((2, 2, rows, pairs), jnp.bfloat16),
            pltpu.VMEM((2, rows, FOLD + LANES), jnp.bfloat16),
            pltpu.VMEM((rows, NLON), jnp.bfloat16),
            pltpu.SemaphoreType.DMA((len(early) + 2,)),
            pltpu.SemaphoreType.DMA((blocks,)),
            pltpu.SemaphoreType.DMA((blocks, 4)),
        ],
        compiler_params=pltpu.CompilerParams(vmem_limit_bytes=52 * 1024 * 1024),
        cost_estimate=pl.CostEstimate(
            flops=8 * rows * pairs * FOLD,
            bytes_accessed=8 * pairs * FOLD + 2 * rows * NLON,
            transcendentals=0,
        ),
        name="fourier",
    )(*early, got, table)


def chunk_counts(slots):
    if slots % (4 * GROUP):
        return (slots,)
    first = slots * 2 // 5 // (2 * GROUP) * (2 * GROUP)
    return (first, slots - first)


def local(spectra, polynomials, wave_order, row_cutoff):
    parts, levels, slots, degrees = spectra.shape
    groups = lax.axis_size("wave")
    shards = lax.axis_size("lev")
    basis = jnp.swapaxes(polynomials, 1, 2)
    counts = chunk_counts(slots)
    got = []
    for chunk, count in enumerate(counts):
        sent = legendre(
            spectra, basis, wave_order, row_cutoff, sum(counts[:chunk]), count, groups * shards
        )
        arrived = lax.all_to_all(sent, ("wave", "lev"), split_axis=0, concat_axis=0, tiled=True)
        got.append(arrived.reshape(groups, shards, 2, count // 2, LANES))
    table = phase_table(wave_order, slots, counts)
    early = [arranged(one, levels) for one in got[:-1]]
    grid = fourier_sum(early, got[-1], table, levels)
    return grid.reshape(LANES // (parts * levels), shards * levels, NLON)


def solution(mesh):
    in_specs = (P(None, "lev", "wave", None), P("wave", None, None), P(), P())
    out_specs = P(("wave", "lev"), None, None)
    return jax.shard_map(local, mesh=mesh, in_specs=in_specs, out_specs=out_specs, check_vma=False)
```

time: 70.2 us -> 67 us (0.954)
  Pallas kernels: 47.7 us -> 42.2 us
  waiting for transfers between devices: 10.9 us -> 12.8 us
  starting transfers between devices: 10.2 us -> 11.6 us
  local copies, waits for them, and re-layouts: 0.86 us -> 0.01 us
    pallas_call x2, Pallas kernels: 18.7 us -> 15.1 us  [the longest x1 7.96 us: fourier_sum(): pl.pallas_call(functools.partial(fourier_kernel, levels=levels, early=len...]
    all_to_all x2, waiting for transfers between devices: 10.9 us -> 12.8 us  [local(): lax.all_to_all(sent, ('wave', 'lev'), split_axis=0, concat_axis=0, tiled=...]
    pallas_call x2, Pallas kernels: 26.5 us -> 24.9 us  [legendre(): pl.pallas_call(functools.partial(legendre_kernel, offset=offset), out_sha...]
    all_to_all x2, starting transfers between devices: 10.2 us -> 11.6 us  [local(): lax.all_to_all(sent, ('wave', 'lev'), split_axis=0, concat_axis=0, tiled=...]
    unnamed x4 -> x2, local copies, waits for them, and re-layouts: 0.86 us -> 0.01 us
  transfers between devices with their start and end apart: 2 -> 2, of which waited for: 2 -> 2; matrix products, arithmetic and copies ran while one was open for 0% -> 0% of each run, Pallas kernels for 36% -> 35%
where the time goes in v3:
time: 67 us; the launch traced here: 66.6 us
  Pallas kernels  42.2 us (63%)
  waiting for transfers between devices  12.8 us (19%)
  starting transfers between devices  11.6 us (17%)
    pallas_call x2, Pallas kernels, legendre(): pl.pallas_call(functools.partial(legendre_kernel, offset=offset), out_sha...  24.9 us
    all_to_all x2, waiting for transfers between devices, local(): lax.all_to_all(sent, ('wave', 'lev'), split_axis=0, concat_axis=0, tiled=...  12.8 us
    all_to_all x2, starting transfers between devices, local(): lax.all_to_all(sent, ('wave', 'lev'), split_axis=0, concat_axis=0, tiled=...  11.6 us
    pallas_call x1, Pallas kernels, fourier_sum(): pl.pallas_call(functools.partial(fourier_kernel, levels=levels, early=len...  7.96 us
    pallas_call x1, Pallas kernels, phase_table(): pl.pallas_call(functools.partial(table_kernel, segments=segments), out_sh...  7.19 us
    pallas_call x1, Pallas kernels, arranged(): pl.pallas_call(functools.partial(arrange_kernel, levels=levels), out_shap...  2.14 us
  transfers between devices with their start and end apart: 2, of which 2 were waited for; matrix products, arithmetic and copies ran while one was open for 0% of the time, Pallas kernels for 35%

profile of v3, /device:TPU:1, one launch (start us, length us, event | category | flops | bytes accessed | tf_op | source)
XLA Modules:
  0.0 66.6 jit_solution(12136570761868589461)
XLA Ops:
  0.0 10.9 %legendre.2 = bf16[32,64,128]{2,1,0:T(8,128)(2,1)} custom-call(s32[1280]{0:T(1024)} %wave_ref.5, s32[64]{0:T(128)} %cut_ref.3, bf16[2,32,160,1280]{3,2,1,0:T(8,128)(2,1)} %coeff_ref.3, bf16[160,32,1280]{2,1,0:T(8,128)(2,1)} %bitcast.5), custom_call_target="tpu_custom_call" | custom-call | flops 5368709120 | bytes 15728640 | tf_op jit(solution)/shard_map/legendre/pallas_call | solution.py:208
  10.9 7.1 %all-to-all-start = ((bf16[32,64,128]{2,1,0:T(8,128)(2,1)}), bf16[32,64,128]{2,1,0:T(8,128)(2,1)S(1)}, u32[]{:S(2)}, u32[]{:S(2)}) async-start(bf16[32,64,128]{2,1,0:T(8,128)(2,1)} %legendre.2), calls=%async_computation | async-start | bytes 1048576 | tf_op jit(solution)/shard_map/all_to_all | solution.py:510
  18.0 14.0 %legendre.3 = bf16[32,96,128]{2,1,0:T(8,128)(2,1)} custom-call(s32[1280]{0:T(1024)} %wave_ref.5, s32[64]{0:T(128)} %cut_ref.3, bf16[2,32,160,1280]{3,2,1,0:T(8,128)(2,1)} %coeff_ref.3, bf16[160,32,1280]{2,1,0:T(8,128)(2,1)} %bitcast.6), custom_call_target="tpu_custom_call" | custom-call | flops 8053063680 | bytes 23592960 | tf_op jit(solution)/shard_map/legendre/pallas_call | solution.py:208
  32.0 1.3 %all-to-all-done = bf16[32,64,128]{2,1,0:T(8,128)(2,1)S(1)} async-done(((bf16[32,64,128]{2,1,0:T(8,128)(2,1)}), bf16[32,64,128]{2,1,0:T(8,128)(2,1)S(1)}, u32[]{:S(2)}, u32[]{:S(2)}) %all-to-all-start) | async-done | bytes 524320 | tf_op jit(solution)/shard_map/all_to_all | solution.py:510
  33.3 0.0 copy-start
  33.3 4.5 %all-to-all-start.1 = ((bf16[32,96,128]{2,1,0:T(8,128)(2,1)}), bf16[32,96,128]{2,1,0:T(8,128)(2,1)S(1)}, u32[]{:S(2)}, u32[]{:S(2)}) async-start(bf16[32,96,128]{2,1,0:T(8,128)(2,1)} %legendre.3), calls=%async_computation.1 | async-start | bytes 1572864 | tf_op jit(solution)/shard_map/all_to_all | solution.py:510
  37.8 7.2 %phases.1.refs_2_ = bf16[6,2,2,640,256]{4,3,2,1,0:T(8,128)(2,1)} custom-call(s32[1280]{0:T(1024)} %wave_ref.5), custom_call_target="tpu_custom_call" | custom-call | flops 26214400 | bytes 6553600 | tf_op jit(solution)/shard_map/phases/pallas_call | solution.py:310
  45.0 0.0 copy-done
  45.0 2.1 %arrange.1.refs_0_ = bf16[24,2,2,256,256]{4,3,2,1,0:T(8,128)(2,1)} custom-call(bf16[8,4,2,32,128]{4,3,2,1,0:T(8,128)(2,1)} %bitcast.7), custom_call_target="tpu_custom_call" | custom-call | flops 67108864 | bytes 1048576 | tf_op jit(solution)/shard_map/arrange/pallas_call | solution.py:355
  47.1 11.5 %all-to-all-done.1 = bf16[32,96,128]{2,1,0:T(8,128)(2,1)S(1)} async-done(((bf16[32,96,128]{2,1,0:T(8,128)(2,1)}), bf16[32,96,128]{2,1,0:T(8,128)(2,1)S(1)}, u32[]{:S(2)}, u32[]{:S(2)}) %all-to-all-start.1) | async-done | bytes 786464 | tf_op jit(solution)/shard_map/all_to_all | solution.py:510
  58.6 8.0 %fourier.1 = bf16[256,5120]{1,0:T(8,128)(2,1)} custom-call(bf16[24,2,2,256,256]{4,3,2,1,0:T(8,128)(2,1)} %arrange.1.refs_0_, bf16[8,4,2,48,128]{4,3,2,1,0:T(8,128)(2,1)S(1)} %bitcast.4, bf16[6,2,2,640,256]{4,3,2,1,0:T(8,128)(2,1)} %phases.1.refs_2_), custom_call_target="tpu_custom_call" | custom-call | flops 1677721600 | bytes 9175040 | tf_op jit(solution)/shard_map/fourier/pallas_call | solution.py:466
Async XLA Ops:
  10.9 22.4 %all-to-all-start = ((bf16[32,64,128]{2,1,0:T(8,128)(2,1)}), bf16[32,64,128]{2,1,0:T(8,128)(2,1)S(1)}, u32[]{:S(2)}, u32[]{:S(2)}) async-start(bf16[32,64,128]{2,1,0:T(8,128)(2,1)} %legendre.2), calls=%async_computation | async-start | bytes 1048576 | tf_op jit(solution)/shard_map/all_to_all | solution.py:510
  33.3 11.7 %copy-start = (bf16[32,64,128]{2,1,0:T(8,128)(2,1)}, bf16[32,64,128]{2,1,0:T(8,128)(2,1)S(1)}, u32[]{:S(2)}) copy-start(bf16[32,64,128]{2,1,0:T(8,128)(2,1)S(1)} %all-to-all-done) | copy-start | bytes 1572868
  33.3 25.4 %all-to-all-start.1 = ((bf16[32,96,128]{2,1,0:T(8,128)(2,1)}), bf16[32,96,128]{2,1,0:T(8,128)(2,1)S(1)}, u32[]{:S(2)}, u32[]{:S(2)}) async-start(bf16[32,96,128]{2,1,0:T(8,128)(2,1)} %legendre.3), calls=%async_computation.1 | async-start | bytes 1572864 | tf_op jit(solution)/shard_map/all_to_all | solution.py:510

commit v4 on v3

--- a/solution.py
+++ b/solution.py
@@ -15,7 +15,6 @@
 WIDTH = 256
 VMEM_LIMIT = 60 * 1024 * 1024
 DEPTH = 3
-ROOM = 24
 
 
 def nt_dot(left, right):
@@ -52,23 +51,17 @@
     cut_ref,
     coeff_ref,
     basis_ref,
-    out_ref,
-    coeff_buffer,
-    basis_buffer,
-    low,
-    high,
-    sums,
-    sort,
-    limits,
-    wide,
-    tall,
-    arrived,
-    *,
+    *refs,
     offset,
+    groups,
+    shards,
 ):
     parts, levels, slots, degrees = coeff_ref.shape
     half = basis_ref.shape[1]
-    targets, count, _ = out_ref.shape
+    out_refs = refs[:-10]
+    coeff_buffer, basis_buffer, low, high, sums, sort, limits, wide, tall, arrived = refs[-10:]
+    count = out_refs[0].shape[1]
+    targets = groups * shards
     batch = sums.shape[0]
     steps = count // (GROUP * batch)
     pairs = GROUP // 2
@@ -194,25 +187,36 @@
     @pl.when(step == steps - 1)
     def _():
         spread(step)
-        out_ref[...] = tall[...].reshape(out_ref.shape).astype(jnp.bfloat16)
-
-
-def legendre(spectra, basis, wave_order, row_cutoff, offset, count, targets):
+        if len(out_refs) == 1:
+            out_refs[0][...] = tall[...].reshape(out_refs[0].shape).astype(jnp.bfloat16)
+            return
+        for shift, out_ref in enumerate(out_refs):
+            for turn in range(groups):
+                target = (lax.axis_index("wave") ^ turn) * shards + (
+                    lax.axis_index("lev") ^ shift
+                )
+                here = pl.ds(pl.multiple_of(target * count, GROUP), count)
+                out_ref[turn] = tall[here, :].astype(jnp.bfloat16)
+
+
+def legendre(spectra, basis, wave_order, row_cutoff, offset, count, groups, shards, relative):
     parts, levels, slots, degrees = spectra.shape
     half = basis.shape[1]
     columns = parts * levels * GROUP
     cut = -(-degrees // 2 // 256) * 256
     batch = 2 if count % (2 * GROUP) == 0 else 1
     steps = count // (batch * GROUP)
+    targets = groups * shards
+    outs, blocks = (shards, groups) if relative else (1, targets)
     anywhere = pl.BlockSpec(memory_space=pl.ANY)
     return pl.pallas_call(
-        functools.partial(legendre_kernel, offset=offset),
-        out_shape=jax.ShapeDtypeStruct((targets, count, LANES), jnp.bfloat16),
+        functools.partial(legendre_kernel, offset=offset, groups=groups, shards=shards),
+        out_shape=[jax.ShapeDtypeStruct((blocks, count, LANES), jnp.bfloat16)] * outs,
         grid_spec=pltpu.PrefetchScalarGridSpec(
             num_scalar_prefetch=2,
             grid=(steps,),
             in_specs=[anywhere, anywhere],
-            out_specs=pl.BlockSpec((targets, count, LANES), lambda g, *_: (0, 0, 0)),
+            out_specs=[pl.BlockSpec((blocks, count, LANES), lambda g, *_: (0, 0, 0))] * outs,
             scratch_shapes=[
                 pltpu.VMEM((DEPTH, batch, parts, levels, GROUP, degrees), jnp.bfloat16),
                 pltpu.VMEM((DEPTH, batch, GROUP, half, degrees), jnp.bfloat16),
@@ -263,7 +267,8 @@
     top = wave_ref.shape[0] - 1
     sublane = lax.broadcasted_iota(jnp.int32, (GROUP, LANES), 0)
     begin = 0
-    for groups, stride, first, pairs in segments:
+    for groups, stride, first, pairs, relative in segments:
+        mask = lax.axis_index("wave") if relative else 0
         lane = lax.broadcasted_iota(jnp.int32, (pairs, LANES), 1).astype(jnp.float32)
 
         @pl.loop(0, groups)
@@ -272,7 +277,7 @@
             for block in range(0, pairs, GROUP):
                 column = jnp.zeros((GROUP, LANES), jnp.int32)
                 for g in range(GROUP):
-                    wave = wave_ref[group * stride + first + 2 * (block + g)]
+                    wave = wave_ref[(group ^ mask) * stride + first + 2 * (block + g)]
                     column = jnp.where(sublane == g, wave, column)
                 waves.append(column)
             column = jnp.concatenate(waves, axis=0)
@@ -301,10 +306,11 @@
     waves = wave_order.shape[0]
     pairs = waves // 2
     if len(counts) == 1:
-        segments = ((waves // 64, 64, 0, 32),)
+        segments = ((waves // 64, 64, 0, 32, False),)
     else:
         segments = tuple(
-            (waves // slots, slots, sum(counts[:n]), count // 2) for n, count in enumerate(counts)
+            (waves // slots, slots, sum(counts[:n]), count // 2, n < len(counts) - 1)
+            for n, count in enumerate(counts)
         )
     blocks = FOLD // WIDTH + 1
     return pl.pallas_call(
@@ -326,61 +332,55 @@
     )(wave_order)
 
 
-def arrange(got_ref, left, levels, begin):
-    groups, shards, _, pairs, _ = got_ref.shape
-    total = groups * pairs
+def repack_kernel(*refs, shards):
+    for turn, out in enumerate(refs[shards:]):
+        for shift in range(shards):
+            out[shift] = refs[shift][turn]
+
+
+def repack(parts):
+    shards = len(parts)
+    groups, count, _ = parts[0].shape
+    return pl.pallas_call(
+        functools.partial(repack_kernel, shards=shards),
+        out_shape=[jax.ShapeDtypeStruct((shards, count, LANES), jnp.bfloat16)] * groups,
+        compiler_params=pltpu.CompilerParams(vmem_limit_bytes=VMEM_LIMIT),
+        cost_estimate=pl.CostEstimate(
+            flops=0, bytes_accessed=4 * groups * shards * count * LANES, transcendentals=0
+        ),
+        name="repack",
+    )(*parts)
+
+
+def arrange(block_of, shard_of, left, total, levels, begin):
+    shards = left.shape[2] * 2 // LANES
     unit = one_hot(
         lax.broadcasted_iota(jnp.int32, (LANES, LANES), 0)
         == lax.broadcasted_iota(jnp.int32, (LANES, LANES), 1)
     )
     for odd in range(2):
         for shard in range(shards):
-            block = got_ref[:, shard, odd].reshape(total, LANES)
-            turned = nt_dot(unit, block).astype(jnp.bfloat16)
+            turned = nt_dot(unit, block_of(shard, odd)).astype(jnp.bfloat16)
             for r in range(LANES // (2 * levels)):
-                here = pl.ds((r * shards + shard) * levels, levels)
+                row = (r * shards + shard_of(shard)) * levels
+                row = row if isinstance(row, int) else pl.multiple_of(row, levels)
+                here = pl.ds(row, levels)
                 for part in range(2):
                     at = (2 * r + part) * levels
                     left[odd, part, here, pl.ds(begin, total)] = turned[at : at + levels, :]
 
 
-def arrange_kernel(got_ref, out_ref, *, levels):
-    arrange(got_ref, out_ref.at[0], levels, 0)
-
-
-def arranged(got, levels):
-    groups, shards, _, pairs, _ = got.shape
-    total = groups * pairs
-    rows = shards * LANES // 2
-    return pl.pallas_call(
-        functools.partial(arrange_kernel, levels=levels),
-        out_shape=jax.ShapeDtypeStruct((ROOM, 2, 2, rows, total), jnp.bfloat16),
-        grid=(1,),
-        in_specs=[pl.BlockSpec(got.shape, lambda g: (0, 0, 0, 0, 0))],
-        out_specs=pl.BlockSpec((1, 2, 2, rows, total), lambda g: (0, 0, 0, 0, 0)),
-        compiler_params=pltpu.CompilerParams(vmem_limit_bytes=VMEM_LIMIT),
-        cost_estimate=pl.CostEstimate(
-            flops=8 * total * rows * LANES, bytes_accessed=16 * total * rows, transcendentals=0
-        ),
-        name="arrange",
-    )(got)
-
-
 def fourier_kernel(*refs, levels, early):
     early_refs = refs[:early]
     got_ref, table_ref, out_ref = refs[early : early + 3]
-    got, table, edge, left, back, result, fetched, arrived, done = refs[early + 3 :]
+    got, sooner, table, edge, left, back, result, fetched, arrived, done = refs[early + 3 :]
     blocks = table_ref.shape[0] - 1
     moves = [pltpu.make_async_copy(got_ref, got, fetched.at[0])]
     edge_move = pltpu.make_async_copy(
         table_ref.at[blocks, :, :, :, pl.ds(0, LANES)], edge, fetched.at[1]
     )
-    begin = 0
     for n, early_ref in enumerate(early_refs):
-        span = early_ref.shape[4]
-        target = left.at[:, :, :, pl.ds(begin, span)]
-        moves.append(pltpu.make_async_copy(early_ref.at[0], target, fetched.at[n + 2]))
-        begin += span
+        moves.append(pltpu.make_async_copy(early_ref, sooner.at[n], fetched.at[n + 2]))
     order = list(range(blocks - 1, -1, -1))
     tables = {
         at: pltpu.make_async_copy(table_ref.at[at], table.at[at], arrived.at[at]) for at in order
@@ -390,10 +390,20 @@
     for at in order:
         tables[at].start()
     edge_move.start()
-    moves[0].wait()
-    arrange(got, left, levels, begin)
-    for move in moves[1:]:
+    for move in moves:
         move.wait()
+    groups, _, _, pairs, _ = got.shape
+    begin = len(early_refs) * sooner.shape[3]
+
+    def sooner_block(shift, odd):
+        return sooner[:, shift, odd].reshape(begin, LANES)
+
+    def got_block(shard, odd):
+        return got[:, shard, odd].reshape(groups * pairs, LANES)
+
+    if early:
+        arrange(sooner_block, lambda shift: lax.axis_index("lev") ^ shift, left, begin, levels, 0)
+    arrange(got_block, lambda shard: shard, left, groups * pairs, levels, begin)
 
     def combine(block):
         sums = [
@@ -470,6 +480,7 @@
         out_specs=anywhere,
         scratch_shapes=[
             pltpu.VMEM(got.shape, jnp.bfloat16),
+            pltpu.VMEM((len(early), *early[0].shape) if early else got.shape, jnp.bfloat16),
             pltpu.VMEM((blocks, *table.shape[1:]), jnp.bfloat16),
             pltpu.VMEM((2, 2, pairs, LANES), jnp.bfloat16),
             pltpu.VMEM((2, 2, rows, pairs), jnp.bfloat16),
@@ -489,10 +500,17 @@
     )(*early, got, table)
 
 
+def swap(block, axis, offset):
+    if offset == 0:
+        return block
+    size = lax.axis_size(axis)
+    return lax.ppermute(block, axis, [(i, i ^ offset) for i in range(size)])
+
+
 def chunk_counts(slots):
     if slots % (4 * GROUP):
         return (slots,)
-    first = slots * 2 // 5 // (2 * GROUP) * (2 * GROUP)
+    first = slots // 2 // (2 * GROUP) * (2 * GROUP)
     return (first, slots - first)
 
 
@@ -502,16 +520,31 @@
     shards = lax.axis_size("lev")
     basis = jnp.swapaxes(polynomials, 1, 2)
     counts = chunk_counts(slots)
-    got = []
+    early = []
+    offset = 0
+    sent = []
+    crossed = []
     for chunk, count in enumerate(counts):
+        last = chunk == len(counts) - 1
+        cutoff, *_ = lax.optimization_barrier((row_cutoff, *sent[:1]))
         sent = legendre(
-            spectra, basis, wave_order, row_cutoff, sum(counts[:chunk]), count, groups * shards
+            spectra, basis, wave_order, cutoff, offset, count, groups, shards, not last
         )
-        arrived = lax.all_to_all(sent, ("wave", "lev"), split_axis=0, concat_axis=0, tiled=True)
-        got.append(arrived.reshape(groups, shards, 2, count // 2, LANES))
+        offset += count
+        if last:
+            block = sent[0]
+            if crossed:
+                block, crossed = lax.optimization_barrier((sent[0], crossed))
+                ready = repack(crossed)
+                here = [swap(one, "wave", turn) for turn, one in enumerate(ready)]
+                here = [one.reshape(shards, 2, counts[0] // 2, LANES) for one in here]
+                early = here
+            got = lax.all_to_all(block, ("wave", "lev"), 0, 0, tiled=True)
+            got = got.reshape(groups, shards, 2, count // 2, LANES)
+        else:
+            crossed = [swap(block, "lev", shift) for shift, block in enumerate(sent)]
     table = phase_table(wave_order, slots, counts)
-    early = [arranged(one, levels) for one in got[:-1]]
-    grid = fourier_sum(early, got[-1], table, levels)
+    grid = fourier_sum(early, got, table, levels)
     return grid.reshape(LANES // (parts * levels), shards * levels, NLON)
 
 

time: 67 us -> 64 us (0.955)
  waiting for transfers between devices: 12.8 us -> 0.03 us
  starting transfers between devices: 11.6 us -> 21.5 us
  Pallas kernels: 42.2 us -> 41.1 us
  local copies, waits for them, and re-layouts: 0.01 us -> 0.89 us
    ppermute x0 -> x10, starting transfers between devices: none -> 13.9 us  [swap(): return lax.ppermute(block, axis, [(i, i ^ offset) for i in range(size)])]
    all_to_all x2 -> x1, waiting for transfers between devices: 12.8 us -> 0.01 us  [local(): got = lax.all_to_all(block, ('wave', 'lev'), 0, 0, tiled=True)]
    all_to_all x2 -> x1, starting transfers between devices: 11.6 us -> 7.6 us  [local(): got = lax.all_to_all(block, ('wave', 'lev'), 0, 0, tiled=True)]
    pallas_call x3, Pallas kernels: 27 us -> 25.8 us  [the longest x2 23.8 us: legendre(): pl.pallas_call(functools.partial(legendre_kernel, offset=offset, groups=g...]
    unnamed x2 -> x8, local copies, waits for them, and re-layouts: 0.01 us -> 0.89 us
  transfers between devices with their start and end apart: 2 -> 11, of which waited for: 2 -> 0; matrix products, arithmetic and copies ran while one was open for 0% -> 0% of each run, Pallas kernels for 35% -> 33%
where the time goes in v4:
time: 64 us; the launch traced here: 63.7 us
  Pallas kernels  41.1 us (64%)
  starting transfers between devices  21.5 us (34%)
  local copies, waits for them, and re-layouts  0.89 us (1%)
    pallas_call x2, Pallas kernels, legendre(): pl.pallas_call(functools.partial(legendre_kernel, offset=offset, groups=g...  23.8 us
    ppermute x10, starting transfers between devices, swap(): return lax.ppermute(block, axis, [(i, i ^ offset) for i in range(size)])  13.9 us
    pallas_call x1, Pallas kernels, fourier_sum(): pl.pallas_call(functools.partial(fourier_kernel, levels=levels, early=len...  8.11 us
    all_to_all x1, starting transfers between devices, local(): got = lax.all_to_all(block, ('wave', 'lev'), 0, 0, tiled=True)  7.6 us
    pallas_call x1, Pallas kernels, phase_table(): pl.pallas_call(functools.partial(table_kernel, segments=segments), out_sh...  7.12 us
    pallas_call x1, Pallas kernels, repack(): pl.pallas_call(functools.partial(repack_kernel, shards=shards), out_shape...  2.04 us
  transfers between devices with their start and end apart: 11, of which 0 were waited for; matrix products, arithmetic and copies ran while one was open for 0% of the time, Pallas kernels for 33%

profile of v4, /device:TPU:1, one launch (start us, length us, event | category | flops | bytes accessed | tf_op | source)
XLA Modules:
  0.0 63.7 jit_solution(2874044718371990083)
XLA Ops:
  0.0 11.9 %legendre.2 = (bf16[8,80,128]{2,1,0:T(8,128)(2,1)}, bf16[8,80,128]{2,1,0:T(8,128)(2,1)}, bf16[8,80,128]{2,1,0:T(8,128)(2,1)}, bf16[8,80,128]{2,1,0:T(8,128)(2,1)}) custom-call(s32[1280]{0:T(1024)} %wave_ref.5, s32[64]{0:T(128)} %cut_ref.1, bf16[2,32,160,1280]{3,2,1,0:T(8,128)(2,1)} %coeff_ref.3, bf16[160,32,1280]{2,1,0:T(8,128)(2,1)} %bitcast.20), custom_call_target="tpu_custom_call" | custom-call | flops 6710886400 | bytes 19660800 | tf_op jit(solution)/shard_map/legendre/pallas_call | solution.py:212
  11.9 2.2 %collective-permute-start = (bf16[8,80,128]{2,1,0:T(8,128)(2,1)}, bf16[8,80,128]{2,1,0:T(8,128)(2,1)S(1)}, u32[]{:S(2)}, u32[]{:S(2)}) collective-permute-start(bf16[8,80,128]{2,1,0:T(8,128)(2,1)} %get-tuple-element.25), channel_id=1, source_target_pairs={{0,1},{1,0},{2,3},{3,2},{4,5},{5,4},{6,7},{7,6},{8,9},{9,8},{10,11... | collective-permute-start | bytes 491528 | tf_op jit(solution)/shard_map/ppermute | solution.py:507
  14.1 2.3 %collective-permute-start.1 = (bf16[8,80,128]{2,1,0:T(8,128)(2,1)}, bf16[8,80,128]{2,1,0:T(8,128)(2,1)S(1)}, u32[]{:S(2)}, u32[]{:S(2)}) collective-permute-start(bf16[8,80,128]{2,1,0:T(8,128)(2,1)} %get-tuple-element.26), channel_id=1, source_target_pairs={{0,2},{1,3},{2,0},{3,1},{4,6},{5,7},{6,4},{7,5},{8,10},{9,11},{10,... | collective-permute-start | bytes 491528 | tf_op jit(solution)/shard_map/ppermute | solution.py:507
  16.4 0.0 collective-permute-start.2
  16.4 11.9 %legendre.3 = bf16[32,80,128]{2,1,0:T(8,128)(2,1)} custom-call(s32[1280]{0:T(1024)} %wave_ref.5, s32[64]{0:T(128)} %cut_ref.1, bf16[2,32,160,1280]{3,2,1,0:T(8,128)(2,1)} %coeff_ref.3, bf16[160,32,1280]{2,1,0:T(8,128)(2,1)} %bitcast.21), custom_call_target="tpu_custom_call" | custom-call | flops 6710886400 | bytes 19660800 | tf_op jit(solution)/shard_map/legendre/pallas_call | solution.py:212
  28.3 0.0 collective-permute-done.refs_1_
  28.3 0.0 copy-start.1
  28.3 0.0 collective-permute-done.1.refs_2_
  28.4 0.0 copy-start.2
  28.4 0.0 collective-permute-done.2.refs_3_
  28.4 0.0 copy-start.3
  28.4 7.6 %all-to-all-start = ((bf16[32,80,128]{2,1,0:T(8,128)(2,1)}), bf16[32,80,128]{2,1,0:T(8,128)(2,1)S(1)}, u32[]{:S(2)}, u32[]{:S(2)}) async-start(bf16[32,80,128]{2,1,0:T(8,128)(2,1)} %legendre.3), calls=%async_computation | async-start | bytes 1310720 | tf_op jit(solution)/shard_map/all_to_all | solution.py:542
  36.0 0.0 copy-done.1
  36.0 0.0 copy-done.2
  36.0 0.0 copy-done.3
  36.0 2.0 %repack.1 = (bf16[4,80,128]{2,1,0:T(8,128)(2,1)}, bf16[4,80,128]{2,1,0:T(8,128)(2,1)}, bf16[4,80,128]{2,1,0:T(8,128)(2,1)}, bf16[4,80,128]{2,1,0:T(8,128)(2,1)},...) custom-call(bf16[8,80,128]{2,1,0:T(8,128)(2,1)} %get-tuple-element.2, ...), custom_call_target="tpu_custom_call" | custom-call | bytes 1310720 | tf_op jit(solution)/shard_map/repack/pallas_call | solution.py:344
  38.1 0.3 collective-permute-start.3
  38.3 1.5 %collective-permute-start.4 = (bf16[4,80,128]{2,1,0:T(8,128)(2,1)}, bf16[4,80,128]{2,1,0:T(8,128)(2,1)S(1)}, u32[]{:S(2)}, u32[]{:S(2)}) collective-permute-start(bf16[4,80,128]{2,1,0:T(8,128)(2,1)} %get-tuple-element.34), channel_id=1, source_target_pairs={{0,8},{4,12},{8,0},{12,4},{16,24},{20,28},{24,16},{28,20},{1,9},{5... | collective-permute-start | bytes 245768 | tf_op jit(solution)/shard_map/ppermute | solution.py:507
  39.8 0.4 collective-permute-start.5
  40.2 1.4 %collective-permute-start.6 = (bf16[4,80,128]{2,1,0:T(8,128)(2,1)}, bf16[4,80,128]{2,1,0:T(8,128)(2,1)S(1)}, u32[]{:S(2)}, u32[]{:S(2)}) collective-permute-start(bf16[4,80,128]{2,1,0:T(8,128)(2,1)} %get-tuple-element.36), channel_id=1, source_target_pairs={{0,16},{4,20},{8,24},{12,28},{16,0},{20,4},{24,8},{28,12},{1,17},{... | collective-permute-start | bytes 245768 | tf_op jit(solution)/shard_map/ppermute | solution.py:507
  41.6 0.3 collective-permute-start.7
  41.9 0.0 collective-permute-done.3
  41.9 2.3 %collective-permute-start.8 = (bf16[4,80,128]{2,1,0:T(8,128)(2,1)}, bf16[4,80,128]{2,1,0:T(8,128)(2,1)S(1)}, u32[]{:S(2)}, u32[]{:S(2)}) collective-permute-start(bf16[4,80,128]{2,1,0:T(8,128)(2,1)} %get-tuple-element.38), channel_id=1, source_target_pairs={{0,24},{4,28},{8,16},{12,20},{16,8},{20,12},{24,0},{28,4},{1,25},{... | collective-permute-start | bytes 245768 | tf_op jit(solution)/shard_map/ppermute | solution.py:507
  44.2 0.0 collective-permute-done.4
  44.2 3.3 %collective-permute-start.9 = (bf16[4,80,128]{2,1,0:T(8,128)(2,1)}, bf16[4,80,128]{2,1,0:T(8,128)(2,1)S(1)}, u32[]{:S(2)}, u32[]{:S(2)}) collective-permute-start(bf16[4,80,128]{2,1,0:T(8,128)(2,1)} %get-tuple-element.39), channel_id=1, source_target_pairs={{0,28},{4,24},{8,20},{12,16},{16,12},{20,8},{24,4},{28,0},{1,29},{... | collective-permute-start | bytes 245768 | tf_op jit(solution)/shard_map/ppermute | solution.py:507
  47.5 7.1 %phases.1.refs_9_ = bf16[6,2,2,640,256]{4,3,2,1,0:T(8,128)(2,1)} custom-call(s32[1280]{0:T(1024)} %wave_ref.5), custom_call_target="tpu_custom_call" | custom-call | flops 26214400 | bytes 6553600 | tf_op jit(solution)/shard_map/phases/pallas_call | solution.py:316
  54.6 0.0 collective-permute-done.5
  54.6 0.0 collective-permute-done.6
  54.6 0.0 collective-permute-done.7
  54.6 0.0 collective-permute-done.8
  54.6 0.0 collective-permute-done.9
  54.7 0.0 all-to-all-done
  54.7 0.0 copy-start
  54.7 0.9 %copy-done = bf16[4,80,128]{2,1,0:T(8,128)(2,1)S(1)} copy-done((bf16[4,80,128]{2,1,0:T(8,128)(2,1)S(1)}, bf16[4,80,128]{2,1,0:T(8,128)(2,1)}, u32[]{:S(2)}) %copy-start) | copy-done | bytes 81944
  55.6 8.1 %fourier.1 = bf16[256,5120]{1,0:T(8,128)(2,1)} custom-call(bf16[4,2,40,128]{3,2,1,0:T(8,128)(2,1)S(1)} %bitcast.12, bf16[4,2,40,128]{3,2,1,0:T(8,128)(2,1)S(1)} %bitcast.13, bf16[4,2,40,128]{3,2,1,0:T(8,128)(2,1)S(1)} %bitcast.14, bf16[4,2,40,128]{3,2,1,0:T(8,128)(2,1)S(1)} %bitcast.15, bf16[4,2,40,128]{3,2,1,0:T(8,128)(2,1)S(1)} %bitcast.16, ...), custom_call_target="tpu_custom_call" | custom-call | flops 1677721600 | bytes 9175040 | tf_op jit(solution)/shard_map/fourier/pallas_call | solution.py:476
Async XLA Ops:
  11.9 16.4 %collective-permute-start = (bf16[8,80,128]{2,1,0:T(8,128)(2,1)}, bf16[8,80,128]{2,1,0:T(8,128)(2,1)S(1)}, u32[]{:S(2)}, u32[]{:S(2)}) collective-permute-start(bf16[8,80,128]{2,1,0:T(8,128)(2,1)} %get-tuple-element.25), channel_id=1, source_target_pairs={{0,1},{1,0},{2,3},{3,2},{4,5},{5,4},{6,7},{7,6},{8,9},{9,8},{10,11... | collective-permute-start | bytes 491528 | tf_op jit(solution)/shard_map/ppermute | solution.py:507
  14.1 14.2 %collective-permute-start.1 = (bf16[8,80,128]{2,1,0:T(8,128)(2,1)}, bf16[8,80,128]{2,1,0:T(8,128)(2,1)S(1)}, u32[]{:S(2)}, u32[]{:S(2)}) collective-permute-start(bf16[8,80,128]{2,1,0:T(8,128)(2,1)} %get-tuple-element.26), channel_id=1, source_target_pairs={{0,2},{1,3},{2,0},{3,1},{4,6},{5,7},{6,4},{7,5},{8,10},{9,11},{10,... | collective-permute-start | bytes 491528 | tf_op jit(solution)/shard_map/ppermute | solution.py:507
  16.4 11.9 %collective-permute-start.2 = (bf16[8,80,128]{2,1,0:T(8,128)(2,1)}, bf16[8,80,128]{2,1,0:T(8,128)(2,1)S(1)}, u32[]{:S(2)}, u32[]{:S(2)}) collective-permute-start(bf16[8,80,128]{2,1,0:T(8,128)(2,1)} %get-tuple-element.27), channel_id=1, source_target_pairs={{0,3},{1,2},{2,1},{3,0},{4,7},{5,6},{6,5},{7,4},{8,11},{9,10},{10,... | collective-permute-start | bytes 491528 | tf_op jit(solution)/shard_map/ppermute | solution.py:507
  28.3 7.7 %copy-start.1 = (bf16[8,80,128]{2,1,0:T(8,128)(2,1)}, bf16[8,80,128]{2,1,0:T(8,128)(2,1)S(1)}, u32[]{:S(2)}) copy-start(bf16[8,80,128]{2,1,0:T(8,128)(2,1)S(1)} %collective-permute-done.refs_1_) | copy-start | bytes 491524
  28.4 7.6 %copy-start.2 = (bf16[8,80,128]{2,1,0:T(8,128)(2,1)}, bf16[8,80,128]{2,1,0:T(8,128)(2,1)S(1)}, u32[]{:S(2)}) copy-start(bf16[8,80,128]{2,1,0:T(8,128)(2,1)S(1)} %collective-permute-done.1.refs_2_) | copy-start | bytes 491524
  28.4 7.6 %copy-start.3 = (bf16[8,80,128]{2,1,0:T(8,128)(2,1)}, bf16[8,80,128]{2,1,0:T(8,128)(2,1)S(1)}, u32[]{:S(2)}) copy-start(bf16[8,80,128]{2,1,0:T(8,128)(2,1)S(1)} %collective-permute-done.2.refs_3_) | copy-start | bytes 491524
  28.4 26.3 %all-to-all-start = ((bf16[32,80,128]{2,1,0:T(8,128)(2,1)}), bf16[32,80,128]{2,1,0:T(8,128)(2,1)S(1)}, u32[]{:S(2)}, u32[]{:S(2)}) async-start(bf16[32,80,128]{2,1,0:T(8,128)(2,1)} %legendre.3), calls=%async_computation | async-start | bytes 1310720 | tf_op jit(solution)/shard_map/all_to_all | solution.py:542
  38.1 3.8 %collective-permute-start.3 = (bf16[4,80,128]{2,1,0:T(8,128)(2,1)}, bf16[4,80,128]{2,1,0:T(8,128)(2,1)S(1)}, u32[]{:S(2)}, u32[]{:S(2)}) collective-permute-start(bf16[4,80,128]{2,1,0:T(8,128)(2,1)} %get-tuple-element.33), channel_id=1, source_target_pairs={{0,4},{4,0},{8,12},{12,8},{16,20},{20,16},{24,28},{28,24},{1,5},{5... | collective-permute-start | bytes 245768 | tf_op jit(solution)/shard_map/ppermute | solution.py:507
  38.3 5.9 %collective-permute-start.4 = (bf16[4,80,128]{2,1,0:T(8,128)(2,1)}, bf16[4,80,128]{2,1,0:T(8,128)(2,1)S(1)}, u32[]{:S(2)}, u32[]{:S(2)}) collective-permute-start(bf16[4,80,128]{2,1,0:T(8,128)(2,1)} %get-tuple-element.34), channel_id=1, source_target_pairs={{0,8},{4,12},{8,0},{12,4},{16,24},{20,28},{24,16},{28,20},{1,9},{5... | collective-permute-start | bytes 245768 | tf_op jit(solution)/shard_map/ppermute | solution.py:507
  39.8 14.8 %collective-permute-start.5 = (bf16[4,80,128]{2,1,0:T(8,128)(2,1)}, bf16[4,80,128]{2,1,0:T(8,128)(2,1)S(1)}, u32[]{:S(2)}, u32[]{:S(2)}) collective-permute-start(bf16[4,80,128]{2,1,0:T(8,128)(2,1)} %get-tuple-element.35), channel_id=1, source_target_pairs={{0,12},{4,8},{8,4},{12,0},{16,28},{20,24},{24,20},{28,16},{1,13},{... | collective-permute-start | bytes 245768 | tf_op jit(solution)/shard_map/ppermute | solution.py:507
  40.2 14.4 %collective-permute-start.6 = (bf16[4,80,128]{2,1,0:T(8,128)(2,1)}, bf16[4,80,128]{2,1,0:T(8,128)(2,1)S(1)}, u32[]{:S(2)}, u32[]{:S(2)}) collective-permute-start(bf16[4,80,128]{2,1,0:T(8,128)(2,1)} %get-tuple-element.36), channel_id=1, source_target_pairs={{0,16},{4,20},{8,24},{12,28},{16,0},{20,4},{24,8},{28,12},{1,17},{... | collective-permute-start | bytes 245768 | tf_op jit(solution)/shard_map/ppermute | solution.py:507
  41.6 13.0 %collective-permute-start.7 = (bf16[4,80,128]{2,1,0:T(8,128)(2,1)}, bf16[4,80,128]{2,1,0:T(8,128)(2,1)S(1)}, u32[]{:S(2)}, u32[]{:S(2)}) collective-permute-start(bf16[4,80,128]{2,1,0:T(8,128)(2,1)} %get-tuple-element.37), channel_id=1, source_target_pairs={{0,20},{4,16},{8,28},{12,24},{16,4},{20,0},{24,12},{28,8},{1,21},{... | collective-permute-start | bytes 245768 | tf_op jit(solution)/shard_map/ppermute | solution.py:507
  41.9 12.7 %collective-permute-start.8 = (bf16[4,80,128]{2,1,0:T(8,128)(2,1)}, bf16[4,80,128]{2,1,0:T(8,128)(2,1)S(1)}, u32[]{:S(2)}, u32[]{:S(2)}) collective-permute-start(bf16[4,80,128]{2,1,0:T(8,128)(2,1)} %get-tuple-element.38), channel_id=1, source_target_pairs={{0,24},{4,28},{8,16},{12,20},{16,8},{20,12},{24,0},{28,4},{1,25},{... | collective-permute-start | bytes 245768 | tf_op jit(solution)/shard_map/ppermute | solution.py:507
  44.2 10.4 %collective-permute-start.9 = (bf16[4,80,128]{2,1,0:T(8,128)(2,1)}, bf16[4,80,128]{2,1,0:T(8,128)(2,1)S(1)}, u32[]{:S(2)}, u32[]{:S(2)}) collective-permute-start(bf16[4,80,128]{2,1,0:T(8,128)(2,1)} %get-tuple-element.39), channel_id=1, source_target_pairs={{0,28},{4,24},{8,20},{12,16},{16,12},{20,8},{24,4},{28,0},{1,29},{... | collective-permute-start | bytes 245768 | tf_op jit(solution)/shard_map/ppermute | solution.py:507
  54.7 0.9 %copy-start = (bf16[4,80,128]{2,1,0:T(8,128)(2,1)S(1)}, bf16[4,80,128]{2,1,0:T(8,128)(2,1)}, u32[]{:S(2)}) copy-start(bf16[4,80,128]{2,1,0:T(8,128)(2,1)} %get-tuple-element.32) | copy-start | bytes 245764
